TPU v7x, 32 devices: a whole 2x2x4 slice. The times are simulated.
32 devices in a mesh: table: 4 (over y, core), cand: 8 (over z, x).
Axes of the slice: x: 2, y: 2, z: 4, core: 2. Of those that a mesh axis runs over, the one named last changes fastest.
Arguments:
- user_feats: bfloat16 [16, 4096], P('cand'), may hold values from -6 to 6
- tower_weight: bfloat16 [4096, 4096], P(None, 'table'), may hold values from -0.09375 to 0.09375
- tower_bias: float32 [4096], P('table'), may hold values from -3 to 3
- user_proj: bfloat16 [4096, 1024], P('table'), may hold values from -0.09375 to 0.09375
- item_ids: int32 [8, 16, 512], P('table', None, 'cand'), may hold values from 0 to 65535, as said below
- tables: bfloat16 [8, 65536, 128], P('table', 'cand'), may hold values from -6 to 6
- cross_weight: bfloat16 [1024, 1024], replicated, may hold values from -0.1875 to 0.1875
- cross_bias: float32 [1024], replicated, may hold values from -1 to 1
- mlp_first: bfloat16 [1024, 4096], P(None, 'table'), may hold values from -0.1875 to 0.1875
- first_bias: float32 [4096], P('table'), may hold values from -3 to 3
- mlp_second: bfloat16 [4096, 1024], P('table'), may hold values from -0.09375 to 0.09375
- second_bias: float32 [1024], replicated, may hold values from -3 to 3
- task_weight: bfloat16 [1024, 8], replicated, may hold values from -0.1875 to 0.1875
- task_bias: float32 [8], replicated, may hold values from -4 to 4
Outputs:
- logits: float32 [8, 16, 512], P(None, 'table', 'cand')
Inputs may be any that keep to these rules, and one draw needn't show every extreme that they name: `item_ids`: rows k * 8192 to (k + 1) * 8192 - 1 of a table lie on index k of cand. For each table and each index of cand, that device's candidates of all requests name at most 256 ids lying on any one index of cand, and exactly 256 for one of them.
All inputs are finite; a program needn't handle non-finite values.
Results may differ from a plain program's by a relative error of at most 0.014.
Values may be sent and summed in bfloat16 or wider, within the bound.
A program may use at most 128 MiB of HBM per device.

v0:
```python
import math

import jax
import jax.numpy as jnp
from jax import lax
from jax.sharding import PartitionSpec as P


def on_device(
    user_feats,
    tower_weight,
    tower_bias,
    user_proj,
    item_ids,
    tables,
    cross_weight,
    cross_bias,
    mlp_first,
    first_bias,
    mlp_second,
    second_bias,
    task_weight,
    task_bias,
):
    n_cand = lax.axis_size("cand")
    n_table = lax.axis_size("table")
    tab_dev, requests, cand_dev = item_ids.shape
    rows_dev = tables.shape[1]
    embed = tables.shape[2]
    capacity = 2 * user_feats.shape[0] * cand_dev
    tower_part = jax.nn.relu(
        jnp.dot(user_feats, tower_weight, preferred_element_type=jnp.float32) + tower_bias
    ).astype(jnp.bfloat16)
    towers = lax.all_gather(tower_part, "cand", axis=0, tiled=True)
    partial_all = jnp.dot(towers, user_proj, preferred_element_type=jnp.float32)
    projected = lax.psum(partial_all.astype(jnp.bfloat16), "table")
    row_total = requests * cand_dev
    block = math.gcd(row_total, 512)
    blocks = row_total // block
    flat_ids = item_ids.reshape(tab_dev, row_total)
    owner_dev = flat_ids // rows_dev
    local_row = flat_ids % rows_dev
    owner_hot = (
        owner_dev[:, :, None] == jnp.arange(n_cand, dtype=jnp.int32)[None, None, :]
    ).astype(jnp.bfloat16)
    blocked_hot = owner_hot.reshape(tab_dev, blocks, block, n_cand)
    lower = (jnp.arange(block)[:, None] >= jnp.arange(block)[None, :]).astype(jnp.bfloat16)
    within = jnp.einsum("ij,tbjo->tbio", lower, blocked_hot, preferred_element_type=jnp.float32)
    hot_wide = blocked_hot.astype(jnp.float32)
    block_totals = jnp.sum(hot_wide, axis=2)
    before = jnp.cumsum(block_totals, axis=1) - block_totals
    running = within + before[:, :, None, :]
    slot_pos = (
        (jnp.sum(running * hot_wide, axis=3) - 1.0).astype(jnp.int32).reshape(tab_dev, row_total)
    )
    flat_slot = owner_dev * capacity + slot_pos
    digits = jnp.stack(
        [local_row % 32, local_row // 32 % 32, local_row // 1024, jnp.ones_like(local_row)], axis=-1
    ).astype(jnp.bfloat16)
    slot_blocks = jnp.transpose(flat_slot.reshape(tab_dev, blocks, block), (1, 0, 2))
    digit_blocks = jnp.transpose(digits.reshape(tab_dev, blocks, block, 4), (1, 0, 2, 3))
    slot_all = jnp.arange(n_cand * capacity, dtype=jnp.int32)

    def place(total, inputs):
        slot_block, digit_block = inputs
        hit = (slot_block[:, :, None] == slot_all[None, None, :]).astype(jnp.bfloat16)
        return (
            total
            + jnp.einsum("tif,tid->tfd", hit, digit_block, preferred_element_type=jnp.float32),
            None,
        )

    placed, _ = lax.scan(
        place, jnp.zeros((tab_dev, n_cand * capacity, 4), jnp.float32), (slot_blocks, digit_blocks)
    )
    value = placed[:, :, 0] + 32.0 * placed[:, :, 1] + 1024.0 * placed[:, :, 2]
    send_rows = jnp.where(placed[:, :, 3] > 0.5, value.astype(jnp.int32), -1)
    send_rows = send_rows.reshape(tab_dev, n_cand, capacity)

    def pick_rows(table_rows, wanted):
        return jnp.take(table_rows, wanted, axis=0)

    safe_rows = jnp.maximum(
        lax.all_to_all(send_rows, "cand", split_axis=1, concat_axis=1, tiled=True), 0
    )
    found = jax.vmap(pick_rows)(tables, safe_rows)
    returned = lax.all_to_all(found, "cand", split_axis=1, concat_axis=1, tiled=True)
    returned = returned.reshape(tab_dev, n_cand * capacity, embed)
    fetched = jnp.take_along_axis(returned, flat_slot[:, :, None], axis=1)
    fetched = jnp.transpose(fetched.reshape(tab_dev, requests, cand_dev, embed), (1, 2, 0, 3))
    fetched = fetched.reshape(requests, cand_dev, tab_dev * embed)
    quarter = requests // n_table
    my_rows = lax.all_to_all(fetched, "table", split_axis=0, concat_axis=2, tiled=True)
    proj_mine = lax.dynamic_slice_in_dim(projected, lax.axis_index("table") * quarter, quarter, 0)
    base = (my_rows.astype(jnp.float32) + proj_mine.astype(jnp.float32)[:, None, :]).astype(
        jnp.bfloat16
    )
    product = jnp.einsum("rcd,de->rce", base, cross_weight, preferred_element_type=jnp.float32)
    base_wide = base.astype(jnp.float32)
    crossed = (base_wide * (product + cross_bias) + base_wide).astype(jnp.bfloat16)
    first_full, bias_full = (
        lax.all_gather(mlp_first, "table", axis=1, tiled=True),
        lax.all_gather(first_bias.astype(jnp.bfloat16), "table", axis=0, tiled=True).astype(
            first_bias.dtype
        ),
    )
    product_first = jnp.einsum(
        "rcd,dh->rch", crossed, first_full, preferred_element_type=jnp.float32
    )
    hidden_full = jax.nn.relu(product_first + bias_full).astype(jnp.bfloat16)
    summed_top = jnp.einsum(
        "rch,ht->rct",
        hidden_full,
        lax.all_gather(mlp_second, "table", axis=0, tiled=True),
        preferred_element_type=jnp.float32,
    )
    top = jax.nn.relu(summed_top + second_bias).astype(jnp.bfloat16)
    scores = jnp.einsum("rct,tk->krc", top, task_weight, preferred_element_type=jnp.float32)
    return scores + task_bias[:, None, None]


def solution(mesh):
    placed = (
        P("cand", None),
        P(None, "table"),
        P("table"),
        P("table", None),
        P("table", None, "cand"),
        P("table", "cand", None),
        P(),
        P(),
        P(None, "table"),
        P("table"),
        P("table", None),
        P(),
        P(),
        P(),
    )
    return jax.shard_map(
        on_device, mesh=mesh, in_specs=placed, out_specs=P(None, "table", "cand"), check_vma=False
    )
```

profile of v0, /device:TPU:14, one launch (start us, length us, event | category | flops | bytes accessed | tf_op | source)
XLA Modules:
  0.0 268.1 jit_solution(8990386175363488802)
XLA Ops:
  6.5 0.0 copy-start
  6.5 0.0 all-gather.4.cloned.1.call-start
  6.5 0.7 all-gather.4.cloned.1.call-update
  7.3 0.0 all-gather.6.cloned.1.call-start
  7.3 0.7 all-gather.6.cloned.1.call-update
  8.0 0.0 copy-done.2
  8.0 0.1 reshape.404
  8.1 0.1 reshape.405
  8.2 0.1 convert_reduce_fusion
  8.3 0.1 pad.3.clone
  8.5 0.1 fusion.78
  8.5 0.1 maximum_bitcast_fusion
  8.6 0.3 fusion.45
  8.9 3.1 %while.11 = (s32[]{:T(128)}, f32[2,2048,4]{1,2,0:T(4,128)S(1)}, s32[2,2,512]{2,0,1:T(2,128)S(1)}, bf16[2,2,512,4]{2,3,1,0:T(4,128)(2,1)S(1)}, s32[]{:T(128)}, /*index=5*/s32[]{:T(128)}) while((s32[]{:T(128)}, f32[2,2048,4]{1,2,0:T(4,128)S(1)}, s32[2,2,512]{2,0,1:T(2,128)S(1)}, bf16[2,2,512,4]{2,3,1,0:T(4,128)(2,1)S(1)}, s32[]{:T(128)}, ...), condition=%wide.region_4.5_spmd.clone, body=%wide.region_3.4_spmd.clone.sunk | while | flops 18907140 | bytes 159831 | solution.py:73
  9.0 1.5 fusion.89
  10.6 1.5 fusion.89
  12.1 0.1 fusion.68
  12.2 10.3 %all_to_all.19 = s32[2,8,256]{2,0,1:T(2,128)S(1)} all-to-all(s32[2,8,256]{2,0,1:T(2,128)S(1)} %bitcast.105), channel_id=1, replica_groups=mesh['table'=4,'cand'=8] {'cand'}, dimensions={1} | all-to-all | bytes 32768 | tf_op jit(solution)/shard_map/all_to_all | solution.py:84
  22.5 107.8 %gather_fusion = bf16[4096,128]{1,0:T(8,128)(2,1)S(1)} fusion(bf16[2,8192,128]{2,1,0:T(8,128)(2,1)} %param.21, s32[4096]{0:T(1024)S(1)} %bitcast.97), kind=kCustom, calls=%fused_computation | custom fusion | bytes 2129920 | tf_op jit(solution)/shard_map/vmap(jit(_take))/gather | solution.py:81
  130.4 0.0 copy-start.3
  130.4 0.0 copy-start.4
  130.4 1.5 copy_select_fusion
  131.9 17.2 %all-to-all-start.1 = ((bf16[2,8,256,128]{3,2,0,1:T(8,128)(2,1)}), bf16[2,8,256,128]{3,2,0,1:T(8,128)(2,1)}, u32[]{:S(2)}, u32[]{:S(2)}) async-start(bf16[2,8,256,128]{3,2,0,1:T(8,128)(2,1)} %copy_select_fusion), calls=%async_computation.1 | async-start | bytes 2097152 | tf_op jit(solution)/shard_map/all_to_all | solution.py:87
  149.1 0.1 reshape.407
  149.2 0.1 convert_element_type.84
  149.4 0.3 copy.31
  149.7 0.0 copy-done.3
  149.7 0.0 copy-done.4
  149.7 0.0 copy-start.5
  149.8 4.6 %fusion.54 = bf16[1,2,1024]{2,1,0:T(2,128)(2,1)S(1)} fusion(bf16[2,4096]{1,0:T(2,128)(2,1)S(1)} %copy-done.3, bf16[4096,1024]{1,0:T(8,128)(2,1)} %param.17, f32[1024]{0:T(1024)S(1)} %copy-done.4), kind=kOutput, calls=%fused_computation.38 | convolution fusion | flops 16783360 | bytes 8413184 | tf_op jit(solution)/shard_map/dot_general | solution.py:32
  154.3 38.5 %all-gather = bf16[8,2,1024]{2,1,0:T(2,128)(2,1)S(1)} all-gather(bf16[1,2,1024]{2,1,0:T(2,128)(2,1)S(1)} %fusion.54), channel_id=1, replica_groups=mesh['table'=4,'cand'=8] {'cand'}, dimensions={0}, use_global_device_ids=true | all-gather | bytes 36864 | tf_op jit(solution)/shard_map/all_gather | solution.py:34
  192.8 0.0 copy-done.5
  192.8 5.2 %all_gather.14 = bf16[4096]{0:T(1024)(128)(2,1)S(1)} all-gather(bf16[1024]{0:T(1024)(128)(2,1)S(1)} %convert_element_type.98), channel_id=1, replica_groups=mesh['table'=4,'cand'=8] {'table'}, dimensions={0}, use_global_device_ids=true | all-gather | bytes 10240 | tf_op jit(solution)/shard_map/all_gather | solution.py:103
  198.0 0.0 all-to-all-done.1
  198.0 1.3 copy.37
  199.3 20.5 %gather_fusion.1 = bf16[2048,128]{1,0:T(8,128)(2,1)} fusion(bf16[2,2048,128]{2,1,0:T(8,128)(2,1)S(1)} %bitcast.99, s32[2048]{0:T(1024)S(1)} %bitcast.98), kind=kCustom, calls=%fused_computation.1 | custom fusion | bytes 1064960 | tf_op jit(solution)/shard_map/jit(take_along_axis)/gather | solution.py:89
  219.8 2.9 %fusion.57 = bf16[16,64,2,128]{3,2,1,0:T(2,128)(2,1)S(1)} fusion(pred[2,16,64]{0,2,1:T(8,128)(4,1)S(1)} %copy.31, bf16[2,16,64,128]{3,2,1,0:T(8,128)(2,1)} %bitcast.103), kind=kLoop, calls=%fused_computation.45 | loop fusion | flops 262144 | bytes 1050624 | tf_op jit(solution)/shard_map/transpose | solution.py:90
  222.7 1.1 reshape.408
  223.9 3.5 %all-to-all-start.2 = ((bf16[16,64,256]{2,1,0:T(8,128)(2,1)}), bf16[16,64,256]{2,1,0:T(8,128)(2,1)S(1)}, u32[]{:S(2)}, u32[]{:S(2)}) async-start(bf16[16,64,256]{2,1,0:T(8,128)(2,1)} %reshape.408), calls=%async_computation.2 | async-start | bytes 1048576 | tf_op jit(solution)/shard_map/all_to_all | solution.py:93
  227.3 2.0 convolution_convert_fusion
  229.3 12.5 %psum.7 = bf16[16,1024]{1,0:T(8,128)(2,1)S(1)} all-reduce(bf16[16,1024]{1,0:T(8,128)(2,1)S(1)} %convolution_convert_fusion), channel_id=1, replica_groups=mesh['table'=4,'cand'=8] {'table'}, use_global_device_ids=true, to_apply=%region_5.6 | all-reduce | flops 16384 | bytes 65536 | tf_op jit(solution)/shard_map/psum | solution.py:36
  241.9 0.0 all-to-all-done.2
  241.9 0.8 copy-done.1
  242.7 1.4 copy.52
  244.1 1.5 reshape.411
  245.7 8.4 %fusion.18 = bf16[4,64,4096]{2,1,0:T(8,128)(2,1)} fusion(bf16[1024,4096]{1,0:T(8,128)(2,1)} %all-gather.4.cloned.1.call-done, f32[4096]{0:T(1024)S(1)} %convert_element_type.99, bf16[1024,1024]{1,0:T(8,128)(2,1)S(1)} %copy-done, f32[4,64,1024]{2,1,0:T(8,128)} %reshape.411, f32[1024]{0:T(1024)S(1)} %copy-done.7, f32[4,1024]{1,0:T(4,128)S(1)} %dynamic-slice_convert_fusion), kind=kOutput, calls=%fused_computation.18 | convolution fusion | flops 2689859584 | bytes 13668352 | tf_op jit(solution)/shard_map/rcd,dh->rch/dot_general | solution.py:107
  254.1 6.5 %fusion.49 = f32[8,4,64]{2,0,1:T(8,128)S(1)} fusion(bf16[4,64,4096]{2,1,0:T(8,128)(2,1)} %fusion.18, bf16[4096,1024]{1,0:T(8,128)(2,1)} %all-gather.6.cloned.1.call-done, f32[1024]{0:T(1024)S(1)} %copy-done.8, bf16[1024,8]{0,1:T(8,128)(2,1)S(1)} %copy-done.6, f32[8]{0:T(128)S(1)} %copy-done.9), kind=kOutput, calls=%fused_computation.34 | convolution fusion | flops 2152466432 | bytes 10514464 | tf_op jit(solution)/shard_map/rct,tk->krc/dot_general | solution.py:118
  260.6 0.6 copy.40
  (37 shorter events, 0.4 us)
Async XLA Ops:
  6.5 239.1 %copy-start = (bf16[1024,1024]{1,0:T(8,128)(2,1)S(1)}, bf16[1024,1024]{1,0:T(8,128)(2,1)}, u32[]{:S(2)}) copy-start(bf16[1024,1024]{1,0:T(8,128)(2,1)} %param.22) | copy-start | bytes 6291460
  6.5 1.5 copy-start.2
  6.5 239.1 %all-gather.4.cloned.1.call-start = ((), (), s32[]{:S(2)}) async-start(), calls=%async_computation.3 | async-start | bytes 10485760 | tf_op jit(solution)/shard_map/all_gather | solution.py:102
  7.3 246.8 %all-gather.6.cloned.1.call-start = ((), (), s32[]{:S(2)}) async-start(), calls=%async_computation.4 | async-start | bytes 10485760 | tf_op jit(solution)/shard_map/all_gather | solution.py:114
  130.4 19.3 %copy-start.3 = (bf16[2,4096]{1,0:T(2,128)(2,1)S(1)}, bf16[2,4096]{1,0:T(2,128)(2,1)}, u32[]{:S(2)}) copy-start(bf16[2,4096]{1,0:T(2,128)(2,1)} %param.16) | copy-start | bytes 49156
  130.4 19.3 %copy-start.4 = (f32[1024]{0:T(1024)S(1)}, f32[1024]{0:T(1024)}, u32[]{:S(2)}) copy-start(f32[1024]{0:T(1024)} %param.18) | copy-start | bytes 12292
  131.9 66.1 %all-to-all-start.1 = ((bf16[2,8,256,128]{3,2,0,1:T(8,128)(2,1)}), bf16[2,8,256,128]{3,2,0,1:T(8,128)(2,1)}, u32[]{:S(2)}, u32[]{:S(2)}) async-start(bf16[2,8,256,128]{3,2,0,1:T(8,128)(2,1)} %copy_select_fusion), calls=%async_computation.1 | async-start | bytes 2097152 | tf_op jit(solution)/shard_map/all_to_all | solution.py:87
  149.7 43.1 %copy-start.5 = (f32[1024]{0:T(1024)S(1)}, f32[1024]{0:T(1024)}, u32[]{:S(2)}) copy-start(f32[1024]{0:T(1024)} %param.25) | copy-start | bytes 12292
  223.9 18.0 %all-to-all-start.2 = ((bf16[16,64,256]{2,1,0:T(8,128)(2,1)}), bf16[16,64,256]{2,1,0:T(8,128)(2,1)S(1)}, u32[]{:S(2)}, u32[]{:S(2)}) async-start(bf16[16,64,256]{2,1,0:T(8,128)(2,1)} %reshape.408), calls=%async_computation.2 | async-start | bytes 1048576 | tf_op jit(solution)/shard_map/all_to_all | solution.py:93
  229.3 16.4 %copy-start.7 = (f32[1024]{0:T(1024)S(1)}, f32[1024]{0:T(1024)}, u32[]{:S(2)}) copy-start(f32[1024]{0:T(1024)} %param.23) | copy-start | bytes 12292
  241.9 0.8 copy-start.1
  245.7 8.4 %copy-start.6 = (bf16[1024,8]{0,1:T(8,128)(2,1)S(1)}, bf16[1024,8]{0,1:T(8,128)(2,1)}, u32[]{:S(2)}) copy-start(bf16[1024,8]{0,1:T(8,128)(2,1)} %param.28) | copy-start | bytes 49156
  245.7 8.4 %copy-start.8 = (f32[1024]{0:T(1024)S(1)}, f32[1024]{0:T(1024)}, u32[]{:S(2)}) copy-start(f32[1024]{0:T(1024)} %param.27) | copy-start | bytes 12292
  245.7 8.4 %copy-start.9 = (f32[8]{0:T(128)S(1)}, f32[8]{0:T(128)}, u32[]{:S(2)}) copy-start(f32[8]{0:T(128)} %param.29) | copy-start | bytes 100
Sparse Core Ops, SparseCore 0:
  8.9 58.4 all-gather.3
  69.0 58.2 all-gather.5
where the time goes:
time: 272 us; the launch traced here: 268 us
  local copies, waits for them, and re-layouts  136 us (50%)
  blocking collectives  66.4 us (24%)
  matrix products  24.8 us (9%)
  starting transfers between devices  20.7 us (8%)
  between operations  13.7 us (5%)
  other arithmetic  5 us (2%)
    gather x2, local copies, waits for them, and re-layouts, pick_rows(): return jnp.take(table_rows, wanted, axis=0)  108 us
    all_gather x1, blocking collectives, on_device(): towers = lax.all_gather(tower_part, 'cand', axis=0, tiled=True)  38.5 us
    gather x1, local copies, waits for them, and re-layouts, on_device(): fetched = jnp.take_along_axis(returned, flat_slot[:, :, None], axis=1)  20.5 us
    all_to_all x1, starting transfers between devices, on_device(): lax.all_to_all(found, 'cand', split_axis=1, concat_axis=1, tiled=True)  17.2 us
    psum x1, blocking collectives, on_device(): projected = lax.psum(partial_all.astype(jnp.bfloat16), 'table')  12.5 us
    all_to_all x1, blocking collectives, on_device(): lax.all_to_all(send_rows, 'cand', split_axis=1, concat_axis=1, tiled=True)  10.3 us
    dot_general x1, matrix products, on_device(): jnp.einsum('rcd,dh->rch', crossed, first_full, preferred_element_type=jnp...  8.39 us
    dot_general x1, matrix products, on_device(): jnp.einsum('rct,tk->krc', top, task_weight, preferred_element_type=jnp.fl...  6.51 us
  transfers between devices with their start and end apart: 4, of which 0 were waited for; matrix products, arithmetic and copies ran while one was open for 59% of the time, Pallas kernels for 0%

commit v1 on v0

v1 whole, which is shorter than its diff:
```python
import functools
import math

import jax
import jax.numpy as jnp
from jax import lax
from jax.experimental import pallas as pl
from jax.experimental.pallas import tpu as pltpu
from jax.sharding import PartitionSpec as P

MESH = pl.DeviceIdType.MESH
VMEM_SPEC = pl.BlockSpec(memory_space=pltpu.VMEM)
SMEM_SPEC = pl.BlockSpec(memory_space=pltpu.SMEM)
ANY_SPEC = pl.BlockSpec(memory_space=pl.ANY)
STEP = 16
LIMIT = 56 << 20


def greet(axis, n):
    me = lax.axis_index(axis)
    barrier = pltpu.get_barrier_semaphore()
    for d in range(1, n):
        pl.semaphore_signal(
            barrier, inc=1, device_id={axis: lax.rem(me + d, n)}, device_id_type=MESH
        )
    pl.semaphore_wait(barrier, n - 1)


def push(src, dst, send, recv, axis, peer):
    return pltpu.make_async_remote_copy(
        src_ref=src,
        dst_ref=dst,
        send_sem=send,
        recv_sem=recv,
        device_id={axis: peer},
        device_id_type=MESH,
    )


def ids_kernel(n, ids_ref, feats_ref, ids_out, feats_out, send, recv):
    me = lax.axis_index("cand")
    greet("cand", n)
    copies = []
    for d in range(1, n):
        peer = lax.rem(me + d, n)
        copies.append(
            push(ids_ref.at[peer], ids_out.at[me], send.at[0, d], recv.at[0, d], "cand", peer)
        )
        copies.append(
            push(feats_ref, feats_out.at[me], send.at[1, d], recv.at[1, d], "cand", peer)
        )
    for copy in copies:
        copy.start()
    ids_out[me] = ids_ref[me]
    feats_out[me] = feats_ref[...]
    for copy in copies:
        copy.wait()


def widen(src, dst, rows):
    size = math.gcd(rows, 256)

    def body(i, carry):
        at = pl.multiple_of(i * size, size)
        dst[pl.ds(at, size), :] = src[pl.ds(at, size), :].astype(jnp.float32)
        return carry

    lax.fori_loop(0, rows // size, body, 0)


def narrow(src, dst, rows):
    size = math.gcd(rows, 256)

    def body(i, carry):
        at = pl.multiple_of(i * size, size)
        dst[pl.ds(at, size), :] = src[pl.ds(at, size), :].astype(jnp.bfloat16)
        return carry

    lax.fori_loop(0, rows // size, body, 0)


def gather_kernel(tab_dev, rows_dev, cap, ids, tab_ref, out_ref, wide, found):
    slots = out_ref.shape[0]
    widen(tab_ref, wide, tab_dev * rows_dev)

    def body(i, carry):
        at = pl.multiple_of(i * STEP, STEP)

        @pl.when(ids[at] >= 0)
        def _():
            for j in range(STEP):
                row = jnp.maximum(ids[at + j], 0)
                found[pl.ds(at + j, 1), :] = wide[pl.ds(row, 1), :]

        return carry

    lax.fori_loop(0, slots // STEP, body, 0)
    narrow(found, out_ref, slots)


def rows_kernel(
    n,
    n_table,
    found,
    feats,
    tower_w,
    tower_b,
    proj_w,
    returned,
    partial,
    w_held,
    p_held,
    send,
    recv,
    load,
):
    me = lax.axis_index("cand")
    w_copy = pltpu.make_async_copy(tower_w, w_held, load.at[0])
    p_copy = pltpu.make_async_copy(proj_w, p_held, load.at[1])
    w_copy.start()
    p_copy.start()
    greet("cand", n)
    copies = []
    for d in range(1, n):
        peer = lax.rem(me + d, n)
        copies.append(
            push(found.at[peer], returned.at[me], send.at[d], recv.at[d], "cand", peer)
        )
    for copy in copies:
        copy.start()
    returned[me] = found[me]
    depth, width = w_held.shape
    chunk = math.gcd(depth, 512)
    w_copy.wait()

    def body(k, acc):
        at = pl.multiple_of(k * chunk, chunk)
        return acc + jnp.dot(
            feats[:, pl.ds(at, chunk)],
            w_held[pl.ds(at, chunk), :],
            preferred_element_type=jnp.float32,
        )

    acc = lax.fori_loop(
        0, depth // chunk, body, jnp.zeros((feats.shape[0], width), jnp.float32)
    )
    tower = jnp.maximum(acc + tower_b[...], 0.0).astype(jnp.bfloat16)
    p_copy.wait()
    part = jnp.dot(tower, p_held[...], preferred_element_type=jnp.float32)
    quarter = partial.shape[1]
    for q in range(n_table):
        partial[q] = part[q * quarter : (q + 1) * quarter, :]
    for copy in copies:
        copy.wait()


def restore_kernel(tab_dev, embed, where, ret_ref, out_ref, wide, fetched):
    rows = out_ref.shape[0]
    widen(ret_ref, wide, wide.shape[0])

    def body(i, carry):
        at = pl.multiple_of(i * STEP, STEP)
        for j in range(STEP):
            fetched[pl.ds(at + j, 1), :] = wide[pl.ds(where[at + j], 1), :]
        return carry

    lax.fori_loop(0, tab_dev * rows // STEP, body, 0)
    for t in range(tab_dev):
        narrow(
            fetched.at[pl.ds(t * rows, rows), :],
            out_ref.at[:, pl.ds(t * embed, embed)],
            rows,
        )


def table_kernel(n, rows_ref, part_ref, bias_ref, mine, parts, biases, send, recv):
    me = lax.axis_index("table")
    count, width = rows_ref.shape[1:]
    greet("table", n)
    copies = []
    for d in range(1, n):
        peer = lax.rem(me + d, n)
        spot = pl.ds(pl.multiple_of(me * width, width), width)
        copies.append(
            push(rows_ref.at[peer], mine.at[:, spot], send.at[0, d], recv.at[0, d], "table", peer)
        )
        copies.append(
            push(part_ref.at[peer], parts.at[me], send.at[1, d], recv.at[1, d], "table", peer)
        )
        copies.append(
            push(bias_ref, biases.at[me], send.at[2, d], recv.at[2, d], "table", peer)
        )
    for copy in copies:
        copy.start()
    mine[:, pl.ds(pl.multiple_of(me * width, width), width)] = rows_ref[me]
    parts[me] = part_ref[me]
    biases[me] = bias_ref[...]
    for copy in copies:
        copy.wait()


def mlp_kernel(
    n_table,
    cand_dev,
    mine,
    parts,
    cross_w,
    cross_b,
    first,
    bias,
    second,
    second_b,
    task_w,
    task_b,
    out,
    crossed,
    acc,
):
    k = pl.program_id(0)

    @pl.when(k == 0)
    def _():
        total = parts[0]
        for q in range(1, n_table):
            total = total + parts[q]
        proj = total.astype(jnp.bfloat16).astype(jnp.float32)
        for r in range(proj.shape[0]):
            span = slice(r * cand_dev, (r + 1) * cand_dev)
            base = (mine[span, :].astype(jnp.float32) + proj[r : r + 1, :]).astype(jnp.bfloat16)
            crossed[span, :] = base
        base = crossed[...]
        wide = base.astype(jnp.float32)
        product = jnp.dot(base, cross_w[...], preferred_element_type=jnp.float32)
        crossed[...] = (wide * (product + cross_b[...]) + wide).astype(jnp.bfloat16)

    hidden = jnp.maximum(
        jnp.dot(crossed[...], first[0], preferred_element_type=jnp.float32) + bias[0], 0.0
    ).astype(jnp.bfloat16)
    term = jnp.dot(hidden, second[0], preferred_element_type=jnp.float32)

    @pl.when(k == 0)
    def _():
        acc[...] = term

    @pl.when(k > 0)
    def _():
        acc[...] += term

    @pl.when(k == n_table - 1)
    def _():
        top = jnp.maximum(acc[...] + second_b[...], 0.0).astype(jnp.bfloat16)
        scores = lax.dot_general(
            task_w[...], top, (((0,), (1,)), ((), ())), preferred_element_type=jnp.float32
        )
        out[...] = scores + task_b[...]


def on_device(
    user_feats,
    tower_weight,
    tower_bias,
    user_proj,
    item_ids,
    tables,
    cross_weight,
    cross_bias,
    mlp_first,
    first_bias,
    mlp_second,
    second_bias,
    task_weight,
    task_bias,
):
    n_cand = lax.axis_size("cand")
    n_table = lax.axis_size("table")
    tab_dev, requests, cand_dev = item_ids.shape
    rows_dev = tables.shape[1]
    embed = tables.shape[2]
    req_dev, user_width = user_feats.shape
    capacity = 2 * req_dev * cand_dev
    first_all = lax.all_gather(mlp_first, "table", axis=0)
    second_all = lax.all_gather(mlp_second, "table", axis=0)

    row_total = requests * cand_dev
    block = math.gcd(row_total, 512)
    blocks = row_total // block
    flat_ids = item_ids.reshape(tab_dev, row_total)
    owner_dev = flat_ids // rows_dev
    local_row = flat_ids % rows_dev
    owner_hot = (
        owner_dev[:, :, None] == jnp.arange(n_cand, dtype=jnp.int32)[None, None, :]
    ).astype(jnp.bfloat16)
    blocked_hot = owner_hot.reshape(tab_dev, blocks, block, n_cand)
    lower = (jnp.arange(block)[:, None] >= jnp.arange(block)[None, :]).astype(jnp.bfloat16)
    within = jnp.einsum("ij,tbjo->tbio", lower, blocked_hot, preferred_element_type=jnp.float32)
    hot_wide = blocked_hot.astype(jnp.float32)
    block_totals = jnp.sum(hot_wide, axis=2)
    before = jnp.cumsum(block_totals, axis=1) - block_totals
    running = within + before[:, :, None, :]
    slot_pos = (
        (jnp.sum(running * hot_wide, axis=3) - 1.0).astype(jnp.int32).reshape(tab_dev, row_total)
    )
    flat_slot = owner_dev * capacity + slot_pos
    digits = jnp.stack(
        [local_row % 32, local_row // 32 % 32, local_row // 1024, jnp.ones_like(local_row)], axis=-1
    ).astype(jnp.bfloat16)
    slot_blocks = jnp.transpose(flat_slot.reshape(tab_dev, blocks, block), (1, 0, 2))
    digit_blocks = jnp.transpose(digits.reshape(tab_dev, blocks, block, 4), (1, 0, 2, 3))
    slot_all = jnp.arange(n_cand * capacity, dtype=jnp.int32)

    def place(total, inputs):
        slot_block, digit_block = inputs
        hit = (slot_block[:, :, None] == slot_all[None, None, :]).astype(jnp.bfloat16)
        return (
            total
            + jnp.einsum("tif,tid->tfd", hit, digit_block, preferred_element_type=jnp.float32),
            None,
        )

    placed, _ = lax.scan(
        place, jnp.zeros((tab_dev, n_cand * capacity, 4), jnp.float32), (slot_blocks, digit_blocks)
    )
    value = placed[:, :, 0] + 32.0 * placed[:, :, 1] + 1024.0 * placed[:, :, 2]
    base_row = jnp.arange(tab_dev, dtype=jnp.int32)[:, None] * rows_dev
    send_rows = jnp.where(placed[:, :, 3] > 0.5, value.astype(jnp.int32) + base_row, -1)
    send_rows = jnp.transpose(send_rows.reshape(tab_dev, n_cand, capacity), (1, 0, 2))

    wanted, feats = pl.pallas_call(
        functools.partial(ids_kernel, n_cand),
        out_shape=(
            jax.ShapeDtypeStruct((n_cand, tab_dev, capacity), jnp.int32),
            jax.ShapeDtypeStruct((n_cand, req_dev, user_width), user_feats.dtype),
        ),
        in_specs=[VMEM_SPEC] * 2,
        out_specs=(VMEM_SPEC,) * 2,
        scratch_shapes=[
            pltpu.SemaphoreType.DMA((2, n_cand)),
            pltpu.SemaphoreType.DMA((2, n_cand)),
        ],
        compiler_params=pltpu.CompilerParams(collective_id=0, has_side_effects=True),
        name="ids",
    )(send_rows, user_feats)

    slots = n_cand * tab_dev * capacity
    found = pl.pallas_call(
        functools.partial(gather_kernel, tab_dev, rows_dev, capacity),
        out_shape=jax.ShapeDtypeStruct((slots, embed), tables.dtype),
        in_specs=[SMEM_SPEC, VMEM_SPEC],
        out_specs=VMEM_SPEC,
        scratch_shapes=[
            pltpu.VMEM((tab_dev * rows_dev, embed), jnp.float32),
            pltpu.VMEM((slots, embed), jnp.float32),
        ],
        compiler_params=pltpu.CompilerParams(vmem_limit_bytes=LIMIT),
        name="gather",
    )(wanted.reshape(slots), tables.reshape(tab_dev * rows_dev, embed))

    returned, partial = pl.pallas_call(
        functools.partial(rows_kernel, n_cand, n_table),
        out_shape=(
            jax.ShapeDtypeStruct((n_cand, tab_dev * capacity, embed), tables.dtype),
            jax.ShapeDtypeStruct((n_table, requests // n_table, user_proj.shape[1]), jnp.float32),
        ),
        in_specs=[VMEM_SPEC, VMEM_SPEC, ANY_SPEC, VMEM_SPEC, ANY_SPEC],
        out_specs=(VMEM_SPEC,) * 2,
        scratch_shapes=[
            pltpu.VMEM(tower_weight.shape, tower_weight.dtype),
            pltpu.VMEM(user_proj.shape, user_proj.dtype),
            pltpu.SemaphoreType.DMA((n_cand,)),
            pltpu.SemaphoreType.DMA((n_cand,)),
            pltpu.SemaphoreType.DMA((2,)),
        ],
        compiler_params=pltpu.CompilerParams(
            collective_id=1, has_side_effects=True, vmem_limit_bytes=LIMIT
        ),
        name="rows",
    )(
        found.reshape(n_cand, tab_dev * capacity, embed),
        feats.reshape(requests, user_width),
        tower_weight,
        tower_bias[None, :],
        user_proj,
    )

    where = (
        owner_dev * (tab_dev * capacity)
        + jnp.arange(tab_dev, dtype=jnp.int32)[:, None] * capacity
        + slot_pos
    )
    fetched = pl.pallas_call(
        functools.partial(restore_kernel, tab_dev, embed),
        out_shape=jax.ShapeDtypeStruct((row_total, tab_dev * embed), tables.dtype),
        in_specs=[SMEM_SPEC, VMEM_SPEC],
        out_specs=VMEM_SPEC,
        scratch_shapes=[
            pltpu.VMEM((slots, embed), jnp.float32),
            pltpu.VMEM((tab_dev * row_total, embed), jnp.float32),
        ],
        compiler_params=pltpu.CompilerParams(vmem_limit_bytes=LIMIT),
        name="restore",
    )(where.reshape(tab_dev * row_total), returned.reshape(slots, embed))

    rows_mine = row_total // n_table
    width = n_table * tab_dev * embed
    mine, parts, biases = pl.pallas_call(
        functools.partial(table_kernel, n_table),
        out_shape=(
            jax.ShapeDtypeStruct((rows_mine, width), tables.dtype),
            jax.ShapeDtypeStruct(partial.shape, jnp.float32),
            jax.ShapeDtypeStruct((n_table, 1, first_bias.shape[0]), jnp.float32),
        ),
        in_specs=[VMEM_SPEC] * 3,
        out_specs=(VMEM_SPEC,) * 3,
        scratch_shapes=[
            pltpu.SemaphoreType.DMA((3, n_table)),
            pltpu.SemaphoreType.DMA((3, n_table)),
        ],
        compiler_params=pltpu.CompilerParams(
            collective_id=2, has_side_effects=True, vmem_limit_bytes=LIMIT
        ),
        name="quarters",
    )(fetched.reshape(n_table, rows_mine, tab_dev * embed), partial, first_bias[None, :])

    tasks = task_weight.shape[1]
    d_top = mlp_second.shape[1]
    whole = lambda a: pl.BlockSpec(a.shape, lambda k: (0,) * a.ndim)
    each = lambda a: pl.BlockSpec((1,) + a.shape[1:], lambda k: (k, 0, 0))
    cross_b, second_b, task_b = cross_bias[None, :], second_bias[None, :], task_bias[:, None]
    logits = pl.pallas_call(
        functools.partial(mlp_kernel, n_table, cand_dev),
        out_shape=jax.ShapeDtypeStruct((tasks, rows_mine), jnp.float32),
        grid=(n_table,),
        in_specs=[
            whole(mine),
            whole(parts),
            whole(cross_weight),
            whole(cross_b),
            each(first_all),
            each(biases),
            each(second_all),
            whole(second_b),
            whole(task_weight),
            whole(task_b),
        ],
        out_specs=pl.BlockSpec((tasks, rows_mine), lambda k: (0, 0)),
        scratch_shapes=[
            pltpu.VMEM((rows_mine, width), jnp.bfloat16),
            pltpu.VMEM((rows_mine, d_top), jnp.float32),
        ],
        compiler_params=pltpu.CompilerParams(vmem_limit_bytes=LIMIT),
        name="mlp",
    )(mine, parts, cross_weight, cross_b, first_all, biases, second_all, second_b, task_weight, task_b)
    return logits.reshape(tasks, requests // n_table, cand_dev)


def solution(mesh):
    placed = (
        P("cand", None),
        P(None, "table"),
        P("table"),
        P("table", None),
        P("table", None, "cand"),
        P("table", "cand", None),
        P(),
        P(),
        P(None, "table"),
        P("table"),
        P("table", None),
        P(),
        P(),
        P(),
    )
    return jax.shard_map(
        on_device, mesh=mesh, in_specs=placed, out_specs=P(None, "table", "cand"), check_vma=False
    )
```

time: 272 us -> 150 us (0.55)
  local copies, waits for them, and re-layouts: 136 us -> 6.29 us
  Pallas kernels: 0 us -> 74 us
  blocking collectives: 66.4 us -> 0 us
  waiting for transfers between devices: 1.41 us -> 49 us
  matrix products: 24.8 us -> 3.34 us
  starting transfers between devices: 20.7 us -> 0.04 us
  other arithmetic: 5 us -> 1.84 us
    gather x3 -> x0, local copies, waits for them, and re-layouts: 128 us -> none  [the longest x2 108 us: pick_rows(): return jnp.take(table_rows, wanted, axis=0)]
    pallas_call x0 -> x6, Pallas kernels: none -> 74 us  [the longest x1 28 us: on_device(): pl.pallas_call(functools.partial(rows_kernel, n_cand, n_table), out_shape...]
    all_gather x2, waiting for transfers between devices: 0.01 us -> 47.6 us  [the longest x1 47.6 us: on_device(): second_all = lax.all_gather(mlp_second, 'table', axis=0)]
    all_gather x2 -> x0, blocking collectives: 43.6 us -> none  [the longest x1 38.5 us: on_device(): towers = lax.all_gather(tower_part, 'cand', axis=0, tiled=True)]
    dot_general x4 -> x0, matrix products: 21.5 us -> none  [the longest x1 8.39 us: on_device(): jnp.einsum('rcd,dh->rch', crossed, first_full, preferred_element_type=jnp...]
    all_to_all x2 -> x0, starting transfers between devices: 20.7 us -> none  [the longest x1 17.2 us: on_device(): lax.all_to_all(found, 'cand', split_axis=1, concat_axis=1, tiled=True)]
    psum x1 -> x0, blocking collectives: 12.5 us -> none  [on_device(): projected = lax.psum(partial_all.astype(jnp.bfloat16), 'table')]
    all_to_all x1 -> x0, blocking collectives: 10.3 us -> none  [on_device(): lax.all_to_all(send_rows, 'cand', split_axis=1, concat_axis=1, tiled=True)]
  transfers between devices with their start and end apart: 4 -> 2, of which waited for: 0 -> 1; matrix products, arithmetic and copies ran while one was open for 59% -> 7% of each run, Pallas kernels for 0% -> 42%
where the time goes in v1:
time: 150 us; the launch traced here: 148 us
  Pallas kernels  74 us (49%)
  waiting for transfers between devices  49 us (33%)
  between operations  13.5 us (9%)
  local copies, waits for them, and re-layouts  6.29 us (4%)
  matrix products  3.34 us (2%)
  other arithmetic  1.84 us (1%)
    all_gather x1, waiting for transfers between devices, on_device(): second_all = lax.all_gather(mlp_second, 'table', axis=0)  47.6 us
    pallas_call x1, Pallas kernels, on_device(): pl.pallas_call(functools.partial(rows_kernel, n_cand, n_table), out_shape...  28 us
    pallas_call x1, Pallas kernels, on_device(): pl.pallas_call(functools.partial(mlp_kernel, n_table, cand_dev), out_shap...  11.3 us
    pallas_call x1, Pallas kernels, on_device(): pl.pallas_call(functools.partial(gather_kernel, tab_dev, rows_dev, capaci...  11.2 us
    pallas_call x1, Pallas kernels, on_device(): pl.pallas_call(functools.partial(table_kernel, n_table), out_shape=(jax.S...  9.69 us
    pallas_call x1, Pallas kernels, on_device(): pl.pallas_call(functools.partial(ids_kernel, n_cand), out_shape=(jax.Shap...  9.29 us
    pallas_call x1, Pallas kernels, on_device(): pl.pallas_call(functools.partial(restore_kernel, tab_dev, embed), out_sha...  4.58 us
    dot_general x2, matrix products, place(): jnp.einsum('tif,tid->tfd', hit, digit_block, preferred_element_type=jnp.f...  3.06 us
  transfers between devices with their start and end apart: 2, of which 1 were waited for; matrix products, arithmetic and copies ran while one was open for 7% of the time, Pallas kernels for 42%

profile of v1, /device:TPU:14, one launch (start us, length us, event | category | flops | bytes accessed | tf_op | source)
XLA Modules:
  0.0 148.1 jit_solution(431454617943777045)
XLA Ops:
  6.5 0.0 copy-start
  6.5 0.0 all-gather.5.cloned.1.call-start
  6.5 0.7 all-gather.5.cloned.1.call-update
  7.3 0.0 all-gather.7.cloned.1.call-start
  7.3 0.7 all-gather.7.cloned.1.call-update
  8.0 0.0 copy-done
  8.0 0.1 reshape.327
  8.1 0.1 reshape.328
  8.2 0.1 reshape.326
  8.3 0.1 convert_reduce_fusion
  8.4 0.1 pad.3.clone
  8.5 0.1 fusion.22
  8.6 0.1 maximum_bitcast_fusion
  8.7 0.3 fusion.10
  9.0 0.0 copy-start.1
  9.0 0.0 copy-start.2
  9.0 3.1 %while.11 = (s32[]{:T(128)}, f32[2,2048,4]{1,2,0:T(4,128)S(1)}, s32[2,2,512]{2,0,1:T(2,128)S(1)}, bf16[2,2,512,4]{2,3,1,0:T(4,128)(2,1)S(1)}, s32[]{:T(128)}, /*index=5*/s32[]{:T(128)}) while((s32[]{:T(128)}, f32[2,2048,4]{1,2,0:T(4,128)S(1)}, s32[2,2,512]{2,0,1:T(2,128)S(1)}, bf16[2,2,512,4]{2,3,1,0:T(4,128)(2,1)S(1)}, s32[]{:T(128)}, ...), condition=%wide.region_4.5_spmd.clone, body=%wide.region_3.4_spmd.clone.sunk | while | flops 18907140 | bytes 159831 | solution.py:320
  9.1 1.5 %fusion.28 = f32[2,2048,4]{1,2,0:T(4,128)S(1)} fusion(s32[2,512]{1,0:T(2,128)S(1)} %bitcast.56, f32[2,2048,4]{1,2,0:T(4,128)S(1)} %get-tuple-element.112, pred[]{:T(512)S(6)} %compare.63, bf16[2,2,512,4]{2,3,1,0:T(4,128)(2,1)S(1)} %get-tuple-element.120, s32[]{:T(128)} %get-tuple-element.111), kind=kOutput, calls=%fused_computation.4.clone.1 | convolution fusion | flops 18907136 | bytes 143365 | tf_op jit(solution)/shard_map/while/body/eval_jaxpr/tif,tid->tfd/dot_general | solution.py:316
  10.7 1.5 %fusion.28 = f32[2,2048,4]{1,2,0:T(4,128)S(1)} fusion(s32[2,512]{1,0:T(2,128)S(1)} %bitcast.56, f32[2,2048,4]{1,2,0:T(4,128)S(1)} %get-tuple-element.112, pred[]{:T(512)S(6)} %compare.63, bf16[2,2,512,4]{2,3,1,0:T(4,128)(2,1)S(1)} %get-tuple-element.120, s32[]{:T(128)} %get-tuple-element.111), kind=kOutput, calls=%fused_computation.4.clone.1 | convolution fusion | flops 18907136 | bytes 143365 | tf_op jit(solution)/shard_map/while/body/eval_jaxpr/tif,tid->tfd/dot_general | solution.py:316
  12.2 0.1 compare_reduce_fusion
  12.3 0.1 convert_reduce_fusion.1
  12.4 0.7 select_bitcast_fusion.ids_ref
  13.0 9.3 %ids.1 = (s32[8,2,256]{2,1,0:T(2,128)}, bf16[8,2,4096]{2,1,0:T(2,128)(2,1)}) custom-call(s32[8,2,256]{2,1,0:T(2,128)} %select_bitcast_fusion.ids_ref, bf16[2,4096]{1,0:T(2,128)(2,1)} %feats_ref.1), custom_call_target="tpu_custom_call" | custom-call | tf_op jit(solution)/shard_map/ids/pallas_call | solution.py:328
  22.3 1.3 copy.28
  23.7 1.6 %reshape.332.feats = bf16[16,4096]{1,0:T(8,128)(2,1)} reshape(bf16[8,2,4096]{2,1,0:T(2,128)(2,1)} %get-tuple-element.41) | data formatting | bytes 262144 | tf_op jit(solution)/shard_map/reshape | solution.py:379
  25.3 0.0 copy-done.1
  25.3 0.9 copy.22.task_w
  26.2 0.0 copy-done.2
  26.2 0.7 copy.23.task_b
  26.8 11.2 %gather.1 = bf16[4096,128]{1,0:T(8,128)(2,1)} custom-call(s32[4096]{0:T(1024)} %bitcast.57, bf16[16384,128]{1,0:T(8,128)(2,1)} %bitcast.52), custom_call_target="tpu_custom_call" | custom-call | tf_op jit(solution)/shard_map/gather/pallas_call | solution.py:345
  38.0 28.0 %rows.1 = (bf16[8,512,128]{2,1,0:T(8,128)(2,1)}, f32[4,4,1024]{2,1,0:T(4,128)}) custom-call(bf16[8,512,128]{2,1,0:T(8,128)(2,1)} %bitcast.53, bf16[16,4096]{1,0:T(8,128)(2,1)} %reshape.332.feats, bf16[4096,1024]{1,0:T(8,128)(2,1)} %tower_w.1, f32[1,1024]{1,0:T(1,128)} %bitcast.62, bf16[1024,1024]{1,0:T(8,128)(2,1)} %proj_w.1), custom_call_target="tpu_custom_call" | custom-call | tf_op jit(solution)/shard_map/rows/pallas_call | solution.py:358
  66.0 0.1 broadcast_bitcast_fusion
  66.1 0.6 fusion.18.where
  66.7 4.6 %restore.1 = bf16[1024,256]{1,0:T(8,128)(2,1)} custom-call(s32[2048]{0:T(1024)} %fusion.18.where, bf16[4096,128]{1,0:T(8,128)(2,1)} %bitcast.55), custom_call_target="tpu_custom_call" | custom-call | tf_op jit(solution)/shard_map/restore/pallas_call | solution.py:390
  71.3 9.7 %quarters.1 = (bf16[256,1024]{1,0:T(8,128)(2,1)}, f32[4,4,1024]{2,1,0:T(4,128)}, f32[4,1,1024]{2,1,0:T(1,128)}) custom-call(bf16[4,256,256]{2,1,0:T(8,128)(2,1)} %bitcast.54, f32[4,4,1024]{2,1,0:T(4,128)} %get-tuple-element.43.part_ref, f32[1,1024]{1,0:T(1,128)} %bitcast.63), custom_call_target="tpu_custom_call" | custom-call | tf_op jit(solution)/shard_map/quarters/pallas_call | solution.py:405
  81.0 0.0 all-gather.5.cloned.1.call-done
  81.0 47.6 %all-gather.7.cloned.1.call-done = bf16[4096,1024]{1,0:T(8,128)(2,1)} async-done(((bf16[1024,1024]{1,0:T(8,128)(2,1)}), bf16[4096,1024]{1,0:T(8,128)(2,1)}) %all-gather.7.cloned.1.call-update) | async-done | bytes 8388624 | tf_op jit(solution)/shard_map/all_gather | solution.py:282
  128.6 11.3 %mlp.1 = f32[8,256]{1,0:T(8,128)} custom-call(bf16[256,1024]{1,0:T(8,128)(2,1)} %get-tuple-element.44.mine, f32[4,4,1024]{2,1,0:T(4,128)} %get-tuple-element.45.parts, bf16[1024,1024]{1,0:T(8,128)(2,1)} %cross_w.1, f32[1,1024]{1,0:T(1,128)} %bitcast.64, bf16[4,1024,1024]{2,1,0:T(8,128)(2,1)} %bitcast.50, f32[4,1,1024]{2,1,0:T(1,128)} %get-tuple-element.46.bias, ...), custom_call_target="tpu_custom_call" | custom-call | tf_op jit(solution)/shard_map/mlp/pallas_call | solution.py:429
  139.9 1.4 reshape.335
  (15 shorter events, 0.2 us)
Async XLA Ops:
  6.5 1.5 copy-start
  6.5 74.5 %all-gather.5.cloned.1.call-start = ((), (), s32[]{:S(2)}) async-start(), calls=%async_computation | async-start | bytes 10485760 | tf_op jit(solution)/shard_map/all_gather | solution.py:281
  7.3 121.3 %all-gather.7.cloned.1.call-start = ((), (), s32[]{:S(2)}) async-start(), calls=%async_computation.1 | async-start | bytes 10485760 | tf_op jit(solution)/shard_map/all_gather | solution.py:282
  9.0 16.3 %copy-start.1 = (bf16[1024,8]{0,1:T(8,128)(2,1)S(1)}, bf16[1024,8]{0,1:T(8,128)(2,1)}, u32[]{:S(2)}) copy-start(bf16[1024,8]{0,1:T(8,128)(2,1)} %param.28) | copy-start | bytes 49156
  9.0 17.1 %copy-start.2 = (f32[8]{0:T(128)S(1)}, f32[8]{0:T(128)}, u32[]{:S(2)}) copy-start(f32[8]{0:T(128)} %param.29) | copy-start | bytes 100
Sparse Core Ops, SparseCore 0:
  8.9 58.5 all-gather.4
  69.0 59.5 all-gather.6

commit v2 on v1

--- a/solution.py
+++ b/solution.py
@@ -13,6 +13,7 @@
 SMEM_SPEC = pl.BlockSpec(memory_space=pltpu.SMEM)
 ANY_SPEC = pl.BlockSpec(memory_space=pl.ANY)
 STEP = 16
+CORES = 2
 LIMIT = 56 << 20
 
 
@@ -106,26 +107,44 @@
     tower_w,
     tower_b,
     proj_w,
+    first,
+    second,
+    bias,
     returned,
     partial,
+    first_o,
+    second_o,
+    bias_o,
     w_held,
     p_held,
     send,
     recv,
+    w_send,
+    w_recv,
     load,
 ):
     me = lax.axis_index("cand")
+    place = lax.axis_index("table")
+    mate = place + 1 - 2 * lax.rem(place, CORES)
     w_copy = pltpu.make_async_copy(tower_w, w_held, load.at[0])
     p_copy = pltpu.make_async_copy(proj_w, p_held, load.at[1])
     w_copy.start()
     p_copy.start()
-    greet("cand", n)
+    barrier = pltpu.get_barrier_semaphore()
+    for d in range(1, n):
+        pl.semaphore_signal(
+            barrier, inc=1, device_id={"cand": lax.rem(me + d, n)}, device_id_type=MESH
+        )
+    pl.semaphore_signal(barrier, inc=1, device_id={"table": mate}, device_id_type=MESH)
+    pl.semaphore_wait(barrier, n)
     copies = []
     for d in range(1, n):
         peer = lax.rem(me + d, n)
         copies.append(
             push(found.at[peer], returned.at[me], send.at[d], recv.at[d], "cand", peer)
         )
+    for i, (src, dst) in enumerate(((first, first_o), (second, second_o), (bias, bias_o))):
+        copies.append(push(src, dst, w_send.at[i], w_recv.at[i], "table", mate))
     for copy in copies:
         copy.start()
     returned[me] = found[me]
@@ -147,9 +166,9 @@
     tower = jnp.maximum(acc + tower_b[...], 0.0).astype(jnp.bfloat16)
     p_copy.wait()
     part = jnp.dot(tower, p_held[...], preferred_element_type=jnp.float32)
-    quarter = partial.shape[1]
+    quarter = partial.shape[2]
     for q in range(n_table):
-        partial[q] = part[q * quarter : (q + 1) * quarter, :]
+        partial[q // CORES, q % CORES] = part[q * quarter : (q + 1) * quarter, :]
     for copy in copies:
         copy.wait()
 
@@ -173,28 +192,36 @@
         )
 
 
-def table_kernel(n, rows_ref, part_ref, bias_ref, mine, parts, biases, send, recv):
+def table_kernel(n, rows_ref, part_ref, mine, parts, send, recv):
     me = lax.axis_index("table")
-    count, width = rows_ref.shape[1:]
+    width = rows_ref.shape[3]
+    spot = pl.ds(pl.multiple_of(me * width, width), width)
     greet("table", n)
     copies = []
     for d in range(1, n):
         peer = lax.rem(me + d, n)
-        spot = pl.ds(pl.multiple_of(me * width, width), width)
+        core = lax.rem(peer, CORES)
         copies.append(
-            push(rows_ref.at[peer], mine.at[:, spot], send.at[0, d], recv.at[0, d], "table", peer)
+            push(
+                rows_ref.at[:, core],
+                mine.at[:, :, spot],
+                send.at[0, d],
+                recv.at[0, d],
+                "table",
+                peer,
+            )
         )
         copies.append(
-            push(part_ref.at[peer], parts.at[me], send.at[1, d], recv.at[1, d], "table", peer)
-        )
-        copies.append(
-            push(bias_ref, biases.at[me], send.at[2, d], recv.at[2, d], "table", peer)
+            push(
+                part_ref.at[:, core], parts.at[me], send.at[1, d], recv.at[1, d], "table", peer
+            )
         )
     for copy in copies:
         copy.start()
-    mine[:, pl.ds(pl.multiple_of(me * width, width), width)] = rows_ref[me]
-    parts[me] = part_ref[me]
-    biases[me] = bias_ref[...]
+    core = lax.rem(me, CORES)
+    for y in range(n // CORES):
+        mine[y, :, spot] = rows_ref[y, core]
+        parts[me, y] = part_ref[y, core]
     for copy in copies:
         copy.wait()
 
@@ -207,52 +234,110 @@
     cross_w,
     cross_b,
     first,
+    first_o,
     bias,
+    bias_o,
     second,
+    second_o,
     second_b,
     task_w,
     task_b,
     out,
+    cross_v,
+    first_v,
+    second_v,
+    base,
     crossed,
     acc,
+    sent,
+    got,
+    load,
+    send,
+    recv,
 ):
-    k = pl.program_id(0)
-
-    @pl.when(k == 0)
-    def _():
-        total = parts[0]
+    me = lax.axis_index("table")
+    core = lax.rem(me, CORES)
+    level = me // CORES
+    levels = n_table // CORES
+    loads = [pltpu.make_async_copy(cross_w, cross_v, load.at[0])]
+    for i, (one, two) in enumerate(((first, second), (first_o, second_o))):
+        loads.append(pltpu.make_async_copy(one, first_v.at[i], load.at[1 + 2 * i]))
+        loads.append(pltpu.make_async_copy(two, second_v.at[i], load.at[2 + 2 * i]))
+    for copy in loads:
+        copy.start()
+    barrier = pltpu.get_barrier_semaphore()
+    for d in range(1, levels):
+        other = lax.rem(level + d, levels) * CORES + core
+        pl.semaphore_signal(barrier, inc=1, device_id={"table": other}, device_id_type=MESH)
+    pl.semaphore_wait(barrier, levels - 1)
+    rows, width = base.shape
+    tile = math.gcd(width, 256)
+    hidden_tile = math.gcd(first.shape[1], 256)
+    biases = (bias, bias_o)
+    copies = []
+    for d in range(1, levels + 1):
+        at_level = lax.rem(level + d, levels)
+        total = parts[0, at_level]
         for q in range(1, n_table):
-            total = total + parts[q]
+            total = total + parts[q, at_level]
         proj = total.astype(jnp.bfloat16).astype(jnp.float32)
         for r in range(proj.shape[0]):
             span = slice(r * cand_dev, (r + 1) * cand_dev)
-            base = (mine[span, :].astype(jnp.float32) + proj[r : r + 1, :]).astype(jnp.bfloat16)
-            crossed[span, :] = base
-        base = crossed[...]
-        wide = base.astype(jnp.float32)
-        product = jnp.dot(base, cross_w[...], preferred_element_type=jnp.float32)
-        crossed[...] = (wide * (product + cross_b[...]) + wide).astype(jnp.bfloat16)
-
-    hidden = jnp.maximum(
-        jnp.dot(crossed[...], first[0], preferred_element_type=jnp.float32) + bias[0], 0.0
-    ).astype(jnp.bfloat16)
-    term = jnp.dot(hidden, second[0], preferred_element_type=jnp.float32)
-
-    @pl.when(k == 0)
-    def _():
-        acc[...] = term
-
-    @pl.when(k > 0)
-    def _():
-        acc[...] += term
-
-    @pl.when(k == n_table - 1)
-    def _():
-        top = jnp.maximum(acc[...] + second_b[...], 0.0).astype(jnp.bfloat16)
-        scores = lax.dot_general(
-            task_w[...], top, (((0,), (1,)), ((), ())), preferred_element_type=jnp.float32
-        )
-        out[...] = scores + task_b[...]
+            base[span, :] = (
+                mine[at_level, span, :].astype(jnp.float32) + proj[r : r + 1, :]
+            ).astype(jnp.bfloat16)
+        if d == 1:
+            loads[0].wait()
+
+        def cross(j, carry):
+            at = pl.ds(pl.multiple_of(j * tile, tile), tile)
+            product = jnp.dot(base[...], cross_v[:, at], preferred_element_type=jnp.float32)
+            wide = base[:, at].astype(jnp.float32)
+            crossed[:, at] = (wide * (product + cross_b[:, at]) + wide).astype(jnp.bfloat16)
+            return carry
+
+        lax.fori_loop(0, width // tile, cross, 0)
+        acc[...] = jnp.zeros_like(acc)
+        for i in range(CORES):
+            if d == 1:
+                loads[1 + 2 * i].wait()
+                loads[2 + 2 * i].wait()
+
+            def layer(j, carry):
+                at = pl.ds(pl.multiple_of(j * hidden_tile, hidden_tile), hidden_tile)
+                hidden = jnp.dot(
+                    crossed[...], first_v[i, :, at], preferred_element_type=jnp.float32
+                )
+                hidden = jnp.maximum(hidden + biases[i][:, at], 0.0).astype(jnp.bfloat16)
+                acc[...] += jnp.dot(
+                    hidden, second_v[i, at, :], preferred_element_type=jnp.float32
+                )
+                return carry
+
+            lax.fori_loop(0, first.shape[1] // hidden_tile, layer, 0)
+        if d < levels:
+            sent[d - 1] = acc[...].astype(jnp.bfloat16)
+            copies.append(
+                push(
+                    sent.at[d - 1],
+                    got.at[d - 1],
+                    send.at[d - 1],
+                    recv.at[d - 1],
+                    "table",
+                    at_level * CORES + core,
+                )
+            )
+            copies[-1].start()
+    for copy in copies:
+        copy.wait()
+    total = acc[...] + second_b[...]
+    for d in range(levels - 1):
+        total = total + got[d].astype(jnp.float32)
+    top = jnp.maximum(total, 0.0).astype(jnp.bfloat16)
+    scores = lax.dot_general(
+        task_w[...], top, (((0,), (1,)), ((), ())), preferred_element_type=jnp.float32
+    )
+    out[...] = scores + task_b[...]
 
 
 def on_device(
@@ -278,9 +363,6 @@
     embed = tables.shape[2]
     req_dev, user_width = user_feats.shape
     capacity = 2 * req_dev * cand_dev
-    first_all = lax.all_gather(mlp_first, "table", axis=0)
-    second_all = lax.all_gather(mlp_second, "table", axis=0)
-
     row_total = requests * cand_dev
     block = math.gcd(row_total, 512)
     blocks = row_total // block
@@ -355,19 +437,28 @@
         name="gather",
     )(wanted.reshape(slots), tables.reshape(tab_dev * rows_dev, embed))
 
-    returned, partial = pl.pallas_call(
+    levels = n_table // CORES
+    bias_row = first_bias[None, :]
+    returned, partial, first_o, second_o, bias_o = pl.pallas_call(
         functools.partial(rows_kernel, n_cand, n_table),
         out_shape=(
             jax.ShapeDtypeStruct((n_cand, tab_dev * capacity, embed), tables.dtype),
-            jax.ShapeDtypeStruct((n_table, requests // n_table, user_proj.shape[1]), jnp.float32),
+            jax.ShapeDtypeStruct(
+                (levels, CORES, requests // n_table, user_proj.shape[1]), jnp.float32
+            ),
+            jax.ShapeDtypeStruct(mlp_first.shape, mlp_first.dtype),
+            jax.ShapeDtypeStruct(mlp_second.shape, mlp_second.dtype),
+            jax.ShapeDtypeStruct(bias_row.shape, bias_row.dtype),
         ),
-        in_specs=[VMEM_SPEC, VMEM_SPEC, ANY_SPEC, VMEM_SPEC, ANY_SPEC],
-        out_specs=(VMEM_SPEC,) * 2,
+        in_specs=[VMEM_SPEC, VMEM_SPEC, ANY_SPEC, VMEM_SPEC, ANY_SPEC, ANY_SPEC, ANY_SPEC, VMEM_SPEC],
+        out_specs=(VMEM_SPEC, VMEM_SPEC, ANY_SPEC, ANY_SPEC, VMEM_SPEC),
         scratch_shapes=[
             pltpu.VMEM(tower_weight.shape, tower_weight.dtype),
             pltpu.VMEM(user_proj.shape, user_proj.dtype),
             pltpu.SemaphoreType.DMA((n_cand,)),
             pltpu.SemaphoreType.DMA((n_cand,)),
+            pltpu.SemaphoreType.DMA((3,)),
+            pltpu.SemaphoreType.DMA((3,)),
             pltpu.SemaphoreType.DMA((2,)),
         ],
         compiler_params=pltpu.CompilerParams(
@@ -380,6 +471,9 @@
         tower_weight,
         tower_bias[None, :],
         user_proj,
+        mlp_first,
+        mlp_second,
+        bias_row,
     )
 
     where = (
@@ -402,54 +496,77 @@
 
     rows_mine = row_total // n_table
     width = n_table * tab_dev * embed
-    mine, parts, biases = pl.pallas_call(
+    mine, parts = pl.pallas_call(
         functools.partial(table_kernel, n_table),
         out_shape=(
-            jax.ShapeDtypeStruct((rows_mine, width), tables.dtype),
-            jax.ShapeDtypeStruct(partial.shape, jnp.float32),
-            jax.ShapeDtypeStruct((n_table, 1, first_bias.shape[0]), jnp.float32),
+            jax.ShapeDtypeStruct((levels, rows_mine, width), tables.dtype),
+            jax.ShapeDtypeStruct((n_table, levels) + partial.shape[2:], jnp.float32),
         ),
-        in_specs=[VMEM_SPEC] * 3,
-        out_specs=(VMEM_SPEC,) * 3,
+        in_specs=[VMEM_SPEC] * 2,
+        out_specs=(VMEM_SPEC,) * 2,
         scratch_shapes=[
-            pltpu.SemaphoreType.DMA((3, n_table)),
-            pltpu.SemaphoreType.DMA((3, n_table)),
+            pltpu.SemaphoreType.DMA((2, n_table)),
+            pltpu.SemaphoreType.DMA((2, n_table)),
         ],
         compiler_params=pltpu.CompilerParams(
             collective_id=2, has_side_effects=True, vmem_limit_bytes=LIMIT
         ),
         name="quarters",
-    )(fetched.reshape(n_table, rows_mine, tab_dev * embed), partial, first_bias[None, :])
+    )(fetched.reshape(levels, CORES, rows_mine, tab_dev * embed), partial)
 
     tasks = task_weight.shape[1]
     d_top = mlp_second.shape[1]
-    whole = lambda a: pl.BlockSpec(a.shape, lambda k: (0,) * a.ndim)
-    each = lambda a: pl.BlockSpec((1,) + a.shape[1:], lambda k: (k, 0, 0))
-    cross_b, second_b, task_b = cross_bias[None, :], second_bias[None, :], task_bias[:, None]
     logits = pl.pallas_call(
         functools.partial(mlp_kernel, n_table, cand_dev),
         out_shape=jax.ShapeDtypeStruct((tasks, rows_mine), jnp.float32),
-        grid=(n_table,),
         in_specs=[
-            whole(mine),
-            whole(parts),
-            whole(cross_weight),
-            whole(cross_b),
-            each(first_all),
-            each(biases),
-            each(second_all),
-            whole(second_b),
-            whole(task_weight),
-            whole(task_b),
-        ],
-        out_specs=pl.BlockSpec((tasks, rows_mine), lambda k: (0, 0)),
+            VMEM_SPEC,
+            VMEM_SPEC,
+            ANY_SPEC,
+            VMEM_SPEC,
+            ANY_SPEC,
+            ANY_SPEC,
+            VMEM_SPEC,
+            VMEM_SPEC,
+            ANY_SPEC,
+            ANY_SPEC,
+            VMEM_SPEC,
+            VMEM_SPEC,
+            VMEM_SPEC,
+        ],
+        out_specs=VMEM_SPEC,
         scratch_shapes=[
+            pltpu.VMEM(cross_weight.shape, cross_weight.dtype),
+            pltpu.VMEM((CORES,) + mlp_first.shape, mlp_first.dtype),
+            pltpu.VMEM((CORES,) + mlp_second.shape, mlp_second.dtype),
+            pltpu.VMEM((rows_mine, width), jnp.bfloat16),
             pltpu.VMEM((rows_mine, width), jnp.bfloat16),
             pltpu.VMEM((rows_mine, d_top), jnp.float32),
-        ],
-        compiler_params=pltpu.CompilerParams(vmem_limit_bytes=LIMIT),
+            pltpu.VMEM((levels - 1, rows_mine, d_top), jnp.bfloat16),
+            pltpu.VMEM((levels - 1, rows_mine, d_top), jnp.bfloat16),
+            pltpu.SemaphoreType.DMA((1 + 2 * CORES,)),
+            pltpu.SemaphoreType.DMA((levels - 1,)),
+            pltpu.SemaphoreType.DMA((levels - 1,)),
+        ],
+        compiler_params=pltpu.CompilerParams(
+            collective_id=3, has_side_effects=True, vmem_limit_bytes=LIMIT
+        ),
         name="mlp",
-    )(mine, parts, cross_weight, cross_b, first_all, biases, second_all, second_b, task_weight, task_b)
+    )(
+        mine,
+        parts,
+        cross_weight,
+        cross_bias[None, :],
+        mlp_first,
+        first_o,
+        bias_row,
+        bias_o,
+        mlp_second,
+        second_o,
+        second_bias[None, :],
+        task_weight,
+        task_bias[:, None],
+    )
     return logits.reshape(tasks, requests // n_table, cand_dev)
 
 

time: 150 us -> 108 us (0.72)
  waiting for transfers between devices: 49 us -> 0 us
  Pallas kernels: 74 us -> 94.7 us
  between operations: 13.5 us -> 0.14 us
    all_gather x2 -> x0, waiting for transfers between devices: 47.6 us -> none  [the longest x1 47.6 us: on_device(): second_all = lax.all_gather(mlp_second, 'table', axis=0)]
    pallas_call x1, Pallas kernels: 11.3 us -> 25.7 us  [on_device(): pl.pallas_call(functools.partial(mlp_kernel, n_table, cand_dev), out_shap...]
    pallas_call x1, Pallas kernels: 9.69 us -> 15.8 us  [on_device(): pl.pallas_call(functools.partial(table_kernel, n_table), out_shape=(jax.S...]
  transfers between devices with their start and end apart: 2 -> 0, of which waited for: 1 -> 0; matrix products, arithmetic and copies ran while one was open for 7% -> 0% of each run, Pallas kernels for 42% -> 0%
where the time goes in v2:
time: 108 us; the launch traced here: 107 us
  Pallas kernels  94.7 us (88%)
  local copies, waits for them, and re-layouts  6.79 us (6%)
  matrix products  3.34 us (3%)
  other arithmetic  1.85 us (2%)
    pallas_call x1, Pallas kernels, on_device(): pl.pallas_call(functools.partial(rows_kernel, n_cand, n_table), out_shape...  28.5 us
    pallas_call x1, Pallas kernels, on_device(): pl.pallas_call(functools.partial(mlp_kernel, n_table, cand_dev), out_shap...  25.7 us
    pallas_call x1, Pallas kernels, on_device(): pl.pallas_call(functools.partial(table_kernel, n_table), out_shape=(jax.S...  15.8 us
    pallas_call x1, Pallas kernels, on_device(): pl.pallas_call(functools.partial(gather_kernel, tab_dev, rows_dev, capaci...  10.9 us
    pallas_call x1, Pallas kernels, on_device(): pl.pallas_call(functools.partial(ids_kernel, n_cand), out_shape=(jax.Shap...  9.29 us
    pallas_call x1, Pallas kernels, on_device(): pl.pallas_call(functools.partial(restore_kernel, tab_dev, embed), out_sha...  4.57 us
    dot_general x2, matrix products, place(): jnp.einsum('tif,tid->tfd', hit, digit_block, preferred_element_type=jnp.f...  3.06 us
    unnamed x13, local copies, waits for them, and re-layouts  2.28 us

profile of v2, /device:TPU:14, one launch (start us, length us, event | category | flops | bytes accessed | tf_op | source)
XLA Modules:
  0.0 106.9 jit_solution(11551952652020017820)
XLA Ops:
  0.0 0.8 reshape.327
  0.8 0.1 convert_reduce_fusion
  1.0 0.3 fusion.10
  1.3 0.8 reshape.328
  2.1 0.1 fusion.22
  2.2 0.1 pad.3.clone
  2.3 0.1 maximum_bitcast_fusion
  2.4 3.1 %while.11 = (s32[]{:T(128)}, f32[2,2048,4]{1,2,0:T(4,128)S(1)}, s32[2,2,512]{2,0,1:T(2,128)S(1)}, bf16[2,2,512,4]{2,3,1,0:T(4,128)(2,1)S(1)}, s32[]{:T(128)}, /*index=5*/s32[]{:T(128)}) while((s32[]{:T(128)}, f32[2,2048,4]{1,2,0:T(4,128)S(1)}, s32[2,2,512]{2,0,1:T(2,128)S(1)}, bf16[2,2,512,4]{2,3,1,0:T(4,128)(2,1)S(1)}, s32[]{:T(128)}, ...), condition=%wide.region_4.5_spmd.clone, body=%wide.region_3.4_spmd.clone.sunk | while | flops 18907140 | bytes 159831 | solution.py:402
  2.4 1.5 %fusion.28 = f32[2,2048,4]{1,2,0:T(4,128)S(1)} fusion(s32[2,512]{1,0:T(2,128)S(1)} %bitcast.52, f32[2,2048,4]{1,2,0:T(4,128)S(1)} %get-tuple-element.116, pred[]{:T(512)S(6)} %compare.63, bf16[2,2,512,4]{2,3,1,0:T(4,128)(2,1)S(1)} %get-tuple-element.124, s32[]{:T(128)} %get-tuple-element.115), kind=kOutput, calls=%fused_computation.4.clone.1 | convolution fusion | flops 18907136 | bytes 143365 | tf_op jit(solution)/shard_map/while/body/eval_jaxpr/tif,tid->tfd/dot_general | solution.py:398
  4.0 1.5 %fusion.28 = f32[2,2048,4]{1,2,0:T(4,128)S(1)} fusion(s32[2,512]{1,0:T(2,128)S(1)} %bitcast.52, f32[2,2048,4]{1,2,0:T(4,128)S(1)} %get-tuple-element.116, pred[]{:T(512)S(6)} %compare.63, bf16[2,2,512,4]{2,3,1,0:T(4,128)(2,1)S(1)} %get-tuple-element.124, s32[]{:T(128)} %get-tuple-element.115), kind=kOutput, calls=%fused_computation.4.clone.1 | convolution fusion | flops 18907136 | bytes 143365 | tf_op jit(solution)/shard_map/while/body/eval_jaxpr/tif,tid->tfd/dot_general | solution.py:398
  5.5 0.1 convert_reduce_fusion.1
  5.6 0.1 compare_reduce_fusion
  5.7 0.7 select_bitcast_fusion.ids_ref
  6.4 9.3 %ids.1 = (s32[8,2,256]{2,1,0:T(2,128)}, bf16[8,2,4096]{2,1,0:T(2,128)(2,1)}) custom-call(s32[8,2,256]{2,1,0:T(2,128)} %select_bitcast_fusion.ids_ref, bf16[2,4096]{1,0:T(2,128)(2,1)} %feats_ref.1), custom_call_target="tpu_custom_call" | custom-call | tf_op jit(solution)/shard_map/ids/pallas_call | solution.py:410
  15.7 1.3 %copy.28 = s32[8,2,2,128]{3,1,2,0:T(2,128)} copy(s32[8,2,2,128]{3,2,1,0:T(2,128)} %bitcast.59) | data formatting | bytes 32768
  17.0 0.0 copy-start.1
  17.0 10.9 %gather.1 = bf16[4096,128]{1,0:T(8,128)(2,1)} custom-call(s32[4096]{0:T(1024)} %bitcast.53, bf16[16384,128]{1,0:T(8,128)(2,1)} %bitcast.49), custom_call_target="tpu_custom_call" | custom-call | tf_op jit(solution)/shard_map/gather/pallas_call | solution.py:427
  27.9 0.0 copy-done.1
  27.9 0.7 reshape.332.feats
  28.6 0.0 copy-start
  28.6 28.5 %rows.1 = (bf16[8,512,128]{2,1,0:T(8,128)(2,1)}, f32[2,2,4,1024]{3,2,1,0:T(4,128)}, bf16[1024,1024]{1,0:T(8,128)(2,1)}, bf16[1024,1024]{1,0:T(8,128)(2,1)}, f32[1,1024]{1,0:T(1,128)}) custom-call(bf16[8,512,128]{2,1,0:T(8,128)(2,1)} %bitcast.48, bf16[16,4096]{1,0:T(8,128)(2,1)} %reshape.332.feats, bf16[4096,1024]{1,0:T(8,128)(2,1)} %tower_w.1, ...), custom_call_target="tpu_custom_call" | custom-call | tf_op jit(solution)/shard_map/rows/pallas_call | solution.py:442
  57.1 0.0 copy-start.2
  57.1 0.0 copy-start.3
  57.2 0.1 broadcast_bitcast_fusion
  57.2 0.0 copy-done
  57.2 0.1 reshape.326
  57.3 0.6 fusion.18.where
  57.9 4.6 %restore.1 = bf16[1024,256]{1,0:T(8,128)(2,1)} custom-call(s32[2048]{0:T(1024)} %fusion.18.where, bf16[4096,128]{1,0:T(8,128)(2,1)} %bitcast.51), custom_call_target="tpu_custom_call" | custom-call | tf_op jit(solution)/shard_map/restore/pallas_call | solution.py:484
  62.5 15.8 %quarters.1 = (bf16[2,256,1024]{2,1,0:T(8,128)(2,1)}, f32[4,2,4,1024]{3,2,1,0:T(4,128)}) custom-call(bf16[2,2,256,256]{3,2,1,0:T(8,128)(2,1)} %bitcast.50, f32[2,2,4,1024]{3,2,1,0:T(4,128)} %get-tuple-element.45.part_ref), custom_call_target="tpu_custom_call" | custom-call | tf_op jit(solution)/shard_map/quarters/pallas_call | solution.py:499
  78.3 0.0 copy-done.2
  78.3 0.8 copy.22.task_w
  79.1 0.0 copy-done.3
  79.1 0.7 copy.23.task_b
  79.8 25.7 %mlp.1 = f32[8,256]{1,0:T(8,128)} custom-call(bf16[2,256,1024]{2,1,0:T(8,128)(2,1)} %get-tuple-element.46.mine, f32[4,2,4,1024]{3,2,1,0:T(4,128)} %get-tuple-element.47.parts, bf16[1024,1024]{1,0:T(8,128)(2,1)} %cross_w.1, f32[1,1024]{1,0:T(1,128)} %bitcast.61, bf16[1024,1024]{1,0:T(8,128)(2,1)} %first.3, bf16[1024,1024]{1,0:T(8,128)(2,1)} %get-tuple-element.48.first_o, ...), custom_call_target="tpu_custom_call" | custom-call | tf_op jit(solution)/shard_map/mlp/pallas_call | solution.py:519
  105.5 1.4 %reshape.335 = f32[8,4,64]{2,1,0:T(4,128)} reshape(f32[8,256]{1,0:T(8,128)} %mlp.1) | data formatting | bytes 16384 | tf_op jit(solution)/shard_map/reshape | solution.py:570
  (15 shorter events, 0.2 us)
Async XLA Ops:
  17.0 10.9 %copy-start.1 = (bf16[8,2,4096]{2,1,0:T(2,128)(2,1)S(1)}, bf16[8,2,4096]{2,1,0:T(2,128)(2,1)}, u32[]{:S(2)}) copy-start(bf16[8,2,4096]{2,1,0:T(2,128)(2,1)} %get-tuple-element.43) | copy-start | bytes 393220
  28.6 28.7 %copy-start = (s32[2,16,64]{2,1,0:T(8,128)S(1)}, s32[2,16,64]{2,1,0:T(8,128)}, u32[]{:S(2)}) copy-start(s32[2,16,64]{2,1,0:T(8,128)} %param.20) | copy-start | bytes 24580
  57.1 21.2 %copy-start.2 = (bf16[1024,8]{0,1:T(8,128)(2,1)S(1)}, bf16[1024,8]{0,1:T(8,128)(2,1)}, u32[]{:S(2)}) copy-start(bf16[1024,8]{0,1:T(8,128)(2,1)} %param.28) | copy-start | bytes 49156
  57.1 22.0 %copy-start.3 = (f32[8]{0:T(128)S(1)}, f32[8]{0:T(128)}, u32[]{:S(2)}) copy-start(f32[8]{0:T(128)} %param.29) | copy-start | bytes 100

commit v3 on v2

--- a/solution.py
+++ b/solution.py
@@ -15,16 +15,6 @@
 STEP = 16
 CORES = 2
 LIMIT = 56 << 20
-
-
-def greet(axis, n):
-    me = lax.axis_index(axis)
-    barrier = pltpu.get_barrier_semaphore()
-    for d in range(1, n):
-        pl.semaphore_signal(
-            barrier, inc=1, device_id={axis: lax.rem(me + d, n)}, device_id_type=MESH
-        )
-    pl.semaphore_wait(barrier, n - 1)
 
 
 def push(src, dst, send, recv, axis, peer):
@@ -38,26 +28,6 @@
     )
 
 
-def ids_kernel(n, ids_ref, feats_ref, ids_out, feats_out, send, recv):
-    me = lax.axis_index("cand")
-    greet("cand", n)
-    copies = []
-    for d in range(1, n):
-        peer = lax.rem(me + d, n)
-        copies.append(
-            push(ids_ref.at[peer], ids_out.at[me], send.at[0, d], recv.at[0, d], "cand", peer)
-        )
-        copies.append(
-            push(feats_ref, feats_out.at[me], send.at[1, d], recv.at[1, d], "cand", peer)
-        )
-    for copy in copies:
-        copy.start()
-    ids_out[me] = ids_ref[me]
-    feats_out[me] = feats_ref[...]
-    for copy in copies:
-        copy.wait()
-
-
 def widen(src, dst, rows):
     size = math.gcd(rows, 256)
 
@@ -80,74 +50,142 @@
     lax.fori_loop(0, rows // size, body, 0)
 
 
-def gather_kernel(tab_dev, rows_dev, cap, ids, tab_ref, out_ref, wide, found):
-    slots = out_ref.shape[0]
-    widen(tab_ref, wide, tab_dev * rows_dev)
-
-    def body(i, carry):
-        at = pl.multiple_of(i * STEP, STEP)
-
-        @pl.when(ids[at] >= 0)
-        def _():
-            for j in range(STEP):
-                row = jnp.maximum(ids[at + j], 0)
-                found[pl.ds(at + j, 1), :] = wide[pl.ds(row, 1), :]
-
-        return carry
-
-    lax.fori_loop(0, slots // STEP, body, 0)
-    narrow(found, out_ref, slots)
-
-
-def rows_kernel(
+def front_kernel(
     n,
     n_table,
-    found,
+    ids,
+    where,
     feats,
+    tab,
     tower_w,
     tower_b,
     proj_w,
     first,
     second,
     bias,
-    returned,
-    partial,
+    mine,
+    parts,
     first_o,
     second_o,
     bias_o,
+    ids_v,
+    ids_s,
+    feats_v,
+    feats_f,
+    tab_v,
+    wide,
+    found,
+    packed,
+    returned,
+    ret_wide,
+    fetched,
+    rows_out,
+    partial,
     w_held,
     p_held,
-    send,
-    recv,
+    load,
+    id_send,
+    id_recv,
+    row_send,
+    row_recv,
     w_send,
     w_recv,
-    load,
+    part_send,
+    part_recv,
+    q_send,
+    q_recv,
 ):
     me = lax.axis_index("cand")
     place = lax.axis_index("table")
-    mate = place + 1 - 2 * lax.rem(place, CORES)
-    w_copy = pltpu.make_async_copy(tower_w, w_held, load.at[0])
-    p_copy = pltpu.make_async_copy(proj_w, p_held, load.at[1])
-    w_copy.start()
-    p_copy.start()
+    core = lax.rem(place, CORES)
+    level = place // CORES
+    levels = n_table // CORES
+    mate = place + 1 - 2 * core
+    tab_copy = pltpu.make_async_copy(tab, tab_v, load.at[0])
+    w_copy = pltpu.make_async_copy(tower_w, w_held, load.at[1])
+    p_copy = pltpu.make_async_copy(proj_w, p_held, load.at[2])
+    tab_copy.start()
     barrier = pltpu.get_barrier_semaphore()
     for d in range(1, n):
         pl.semaphore_signal(
             barrier, inc=1, device_id={"cand": lax.rem(me + d, n)}, device_id_type=MESH
         )
-    pl.semaphore_signal(barrier, inc=1, device_id={"table": mate}, device_id_type=MESH)
-    pl.semaphore_wait(barrier, n)
-    copies = []
-    for d in range(1, n):
+    for d in range(1, n_table):
+        pl.semaphore_signal(
+            barrier,
+            inc=1,
+            device_id={"table": lax.rem(place + d, n_table)},
+            device_id_type=MESH,
+        )
+    pl.semaphore_wait(barrier, n + n_table - 2)
+
+    def id_copy(d):
         peer = lax.rem(me + d, n)
-        copies.append(
-            push(found.at[peer], returned.at[me], send.at[d], recv.at[d], "cand", peer)
-        )
-    for i, (src, dst) in enumerate(((first, first_o), (second, second_o), (bias, bias_o))):
-        copies.append(push(src, dst, w_send.at[i], w_recv.at[i], "table", mate))
-    for copy in copies:
+        return push(ids.at[peer], ids_v.at[me], id_send.at[0, d], id_recv.at[0, d], "cand", peer)
+
+    def feat_copy(d):
+        peer = lax.rem(me + d, n)
+        return push(feats, feats_v.at[me], id_send.at[1, d], id_recv.at[1, d], "cand", peer)
+
+    def row_copy(d):
+        peer = lax.rem(me + d, n)
+        return push(packed.at[peer], returned.at[me], row_send.at[d], row_recv.at[d], "cand", peer)
+
+    def each(low, high, act):
+        def body(d, carry):
+            act(d)
+            return carry
+
+        lax.fori_loop(low, high, body, 0)
+
+    each(1, n, lambda d: id_copy(d).start())
+    each(1, n, lambda d: feat_copy(d).start())
+    swaps = [
+        push(src, dst, w_send.at[i], w_recv.at[i], "table", mate)
+        for i, (src, dst) in enumerate(((first, first_o), (second, second_o), (bias, bias_o)))
+    ]
+    for copy in swaps:
         copy.start()
-    returned[me] = found[me]
+    ids_v[me] = ids[me]
+    feats_v[me] = feats[...]
+    tab_copy.wait()
+    w_copy.start()
+    p_copy.start()
+    widen(tab_v, wide, wide.shape[0])
+    each(1, n, lambda d: id_copy(d).wait())
+    to_scalar = pltpu.make_async_copy(ids_v, ids_s, load.at[3])
+    to_scalar.start()
+    to_scalar.wait()
+
+    per = found.shape[0]
+    lanes = ids_s.shape[2]
+
+    def gather(d, out):
+        peer = lax.rem(me + d, n)
+
+        def body(i, carry):
+            at = pl.multiple_of(i * STEP, STEP)
+            line = i // (lanes // STEP)
+            spot = lax.rem(i, lanes // STEP) * STEP
+            for j in range(STEP):
+                row = jnp.maximum(ids_s[peer, line, spot + j], 0)
+                found[pl.ds(at + j, 1), :] = wide[pl.ds(row, 1), :]
+            return carry
+
+        lax.fori_loop(0, per // STEP, body, 0)
+        narrow(found, out.at[peer], per)
+
+    def serve(d):
+        gather(d, packed)
+        row_copy(d).start()
+
+    each(1, n, serve)
+    gather(0, returned)
+
+    each(1, n, lambda d: feat_copy(d).wait())
+    step = feats.shape[0]
+    for c in range(n):
+        feats_f[c * step : (c + 1) * step, :] = feats_v[c].astype(jnp.float32)
     depth, width = w_held.shape
     chunk = math.gcd(depth, 512)
     w_copy.wait()
@@ -155,13 +193,13 @@
     def body(k, acc):
         at = pl.multiple_of(k * chunk, chunk)
         return acc + jnp.dot(
-            feats[:, pl.ds(at, chunk)],
+            feats_f[:, pl.ds(at, chunk)].astype(jnp.bfloat16),
             w_held[pl.ds(at, chunk), :],
             preferred_element_type=jnp.float32,
         )
 
     acc = lax.fori_loop(
-        0, depth // chunk, body, jnp.zeros((feats.shape[0], width), jnp.float32)
+        0, depth // chunk, body, jnp.zeros((feats_f.shape[0], width), jnp.float32)
     )
     tower = jnp.maximum(acc + tower_b[...], 0.0).astype(jnp.bfloat16)
     p_copy.wait()
@@ -169,60 +207,80 @@
     quarter = partial.shape[2]
     for q in range(n_table):
         partial[q // CORES, q % CORES] = part[q * quarter : (q + 1) * quarter, :]
-    for copy in copies:
-        copy.wait()
-
-
-def restore_kernel(tab_dev, embed, where, ret_ref, out_ref, wide, fetched):
-    rows = out_ref.shape[0]
-    widen(ret_ref, wide, wide.shape[0])
-
-    def body(i, carry):
-        at = pl.multiple_of(i * STEP, STEP)
-        for j in range(STEP):
-            fetched[pl.ds(at + j, 1), :] = wide[pl.ds(where[at + j], 1), :]
-        return carry
-
-    lax.fori_loop(0, tab_dev * rows // STEP, body, 0)
-    for t in range(tab_dev):
-        narrow(
-            fetched.at[pl.ds(t * rows, rows), :],
-            out_ref.at[:, pl.ds(t * embed, embed)],
-            rows,
-        )
-
-
-def table_kernel(n, rows_ref, part_ref, mine, parts, send, recv):
-    me = lax.axis_index("table")
-    width = rows_ref.shape[3]
-    spot = pl.ds(pl.multiple_of(me * width, width), width)
-    greet("table", n)
-    copies = []
-    for d in range(1, n):
-        peer = lax.rem(me + d, n)
-        core = lax.rem(peer, CORES)
-        copies.append(
+
+    part_copies = []
+    for d in range(1, n_table):
+        peer = lax.rem(place + d, n_table)
+        part_copies.append(
             push(
-                rows_ref.at[:, core],
-                mine.at[:, :, spot],
-                send.at[0, d],
-                recv.at[0, d],
+                partial.at[:, lax.rem(peer, CORES)],
+                parts.at[place],
+                part_send.at[d],
+                part_recv.at[d],
                 "table",
                 peer,
             )
         )
-        copies.append(
-            push(
-                part_ref.at[:, core], parts.at[me], send.at[1, d], recv.at[1, d], "table", peer
-            )
-        )
-    for copy in copies:
+    for copy in part_copies:
         copy.start()
-    core = lax.rem(me, CORES)
-    for y in range(n // CORES):
-        mine[y, :, spot] = rows_ref[y, core]
-        parts[me, y] = part_ref[y, core]
-    for copy in copies:
+    for y in range(levels):
+        parts[place, y] = partial[y, core]
+
+    def arrive(d):
+        @pl.when(d > 0)
+        def _():
+            row_copy(d).wait()
+
+        source = lax.rem(me - d + n, n)
+        at = pl.multiple_of(source * per, per)
+        widen(returned.at[source], ret_wide.at[pl.ds(at, per), :], per)
+
+    each(0, n, arrive)
+
+    count = rows_out.shape[2]
+    embed = wide.shape[1]
+    tab_dev = rows_out.shape[3] // embed
+    share = tab_dev * embed
+    lane = pl.ds(pl.multiple_of(place * share, share), share)
+    rows = n_table * count
+    quarter_copies = []
+    for turn in range(CORES - 1, -1, -1):
+        target = lax.rem(core + turn, CORES)
+        for y in range(levels):
+            begin = (y * CORES + target) * count
+
+            for t in range(tab_dev):
+
+                def restore(i, carry):
+                    at = pl.multiple_of(i * STEP, STEP)
+                    for j in range(STEP):
+                        fetched[pl.ds(at + j, 1), :] = wide_row(t * rows + begin + at + j)
+                    return carry
+
+                def wide_row(i):
+                    return ret_wide[pl.ds(where[i], 1), :]
+
+                lax.fori_loop(0, count // STEP, restore, 0)
+                narrow(
+                    fetched, rows_out.at[y, target, :, pl.ds(t * embed, embed)], count
+                )
+            for up in range(levels - 1, -1, -1):
+                if turn == 0 and up == 0:
+                    mine[y, :, lane] = rows_out[y, target]
+                    continue
+                peer = lax.rem(level + up, levels) * CORES + target
+                spot = turn * levels + up
+                copy = push(
+                    rows_out.at[y, target],
+                    mine.at[y, :, lane],
+                    q_send.at[spot, y],
+                    q_recv.at[spot, y],
+                    "table",
+                    peer,
+                )
+                copy.start()
+                quarter_copies.append(copy)
+    for copy in quarter_copies + part_copies + swaps:
         copy.wait()
 
 
@@ -407,67 +465,81 @@
     send_rows = jnp.where(placed[:, :, 3] > 0.5, value.astype(jnp.int32) + base_row, -1)
     send_rows = jnp.transpose(send_rows.reshape(tab_dev, n_cand, capacity), (1, 0, 2))
 
-    wanted, feats = pl.pallas_call(
-        functools.partial(ids_kernel, n_cand),
-        out_shape=(
-            jax.ShapeDtypeStruct((n_cand, tab_dev, capacity), jnp.int32),
-            jax.ShapeDtypeStruct((n_cand, req_dev, user_width), user_feats.dtype),
-        ),
-        in_specs=[VMEM_SPEC] * 2,
-        out_specs=(VMEM_SPEC,) * 2,
-        scratch_shapes=[
-            pltpu.SemaphoreType.DMA((2, n_cand)),
-            pltpu.SemaphoreType.DMA((2, n_cand)),
-        ],
-        compiler_params=pltpu.CompilerParams(collective_id=0, has_side_effects=True),
-        name="ids",
-    )(send_rows, user_feats)
-
+    where = (
+        owner_dev * (tab_dev * capacity)
+        + jnp.arange(tab_dev, dtype=jnp.int32)[:, None] * capacity
+        + slot_pos
+    )
     slots = n_cand * tab_dev * capacity
-    found = pl.pallas_call(
-        functools.partial(gather_kernel, tab_dev, rows_dev, capacity),
-        out_shape=jax.ShapeDtypeStruct((slots, embed), tables.dtype),
-        in_specs=[SMEM_SPEC, VMEM_SPEC],
-        out_specs=VMEM_SPEC,
-        scratch_shapes=[
-            pltpu.VMEM((tab_dev * rows_dev, embed), jnp.float32),
-            pltpu.VMEM((slots, embed), jnp.float32),
-        ],
-        compiler_params=pltpu.CompilerParams(vmem_limit_bytes=LIMIT),
-        name="gather",
-    )(wanted.reshape(slots), tables.reshape(tab_dev * rows_dev, embed))
-
+    per = tab_dev * capacity
+    lanes = math.gcd(per, 128)
     levels = n_table // CORES
     bias_row = first_bias[None, :]
-    returned, partial, first_o, second_o, bias_o = pl.pallas_call(
-        functools.partial(rows_kernel, n_cand, n_table),
+    quarter = requests // n_table
+    rows_mine = row_total // n_table
+    width = n_table * tab_dev * embed
+    parts_shape = (levels, quarter, user_proj.shape[1])
+    vmem = pltpu.VMEM
+    dma = pltpu.SemaphoreType.DMA
+    mine, parts, first_o, second_o, bias_o = pl.pallas_call(
+        functools.partial(front_kernel, n_cand, n_table),
         out_shape=(
-            jax.ShapeDtypeStruct((n_cand, tab_dev * capacity, embed), tables.dtype),
-            jax.ShapeDtypeStruct(
-                (levels, CORES, requests // n_table, user_proj.shape[1]), jnp.float32
-            ),
+            jax.ShapeDtypeStruct((levels, rows_mine, width), tables.dtype),
+            jax.ShapeDtypeStruct((n_table,) + parts_shape, jnp.float32),
             jax.ShapeDtypeStruct(mlp_first.shape, mlp_first.dtype),
             jax.ShapeDtypeStruct(mlp_second.shape, mlp_second.dtype),
             jax.ShapeDtypeStruct(bias_row.shape, bias_row.dtype),
         ),
-        in_specs=[VMEM_SPEC, VMEM_SPEC, ANY_SPEC, VMEM_SPEC, ANY_SPEC, ANY_SPEC, ANY_SPEC, VMEM_SPEC],
+        in_specs=[
+            VMEM_SPEC,
+            SMEM_SPEC,
+            VMEM_SPEC,
+            ANY_SPEC,
+            ANY_SPEC,
+            VMEM_SPEC,
+            ANY_SPEC,
+            ANY_SPEC,
+            ANY_SPEC,
+            VMEM_SPEC,
+        ],
         out_specs=(VMEM_SPEC, VMEM_SPEC, ANY_SPEC, ANY_SPEC, VMEM_SPEC),
         scratch_shapes=[
-            pltpu.VMEM(tower_weight.shape, tower_weight.dtype),
-            pltpu.VMEM(user_proj.shape, user_proj.dtype),
-            pltpu.SemaphoreType.DMA((n_cand,)),
-            pltpu.SemaphoreType.DMA((n_cand,)),
-            pltpu.SemaphoreType.DMA((3,)),
-            pltpu.SemaphoreType.DMA((3,)),
-            pltpu.SemaphoreType.DMA((2,)),
+            vmem((n_cand, per // lanes, lanes), jnp.int32),
+            pltpu.SMEM((n_cand, per // lanes, lanes), jnp.int32),
+            vmem((n_cand, req_dev, user_width), user_feats.dtype),
+            vmem((requests, user_width), jnp.float32),
+            vmem((tab_dev * rows_dev, embed), tables.dtype),
+            vmem((tab_dev * rows_dev, embed), jnp.float32),
+            vmem((per, embed), jnp.float32),
+            vmem((n_cand, per, embed), tables.dtype),
+            vmem((n_cand, per, embed), tables.dtype),
+            vmem((slots, embed), jnp.float32),
+            vmem((rows_mine, embed), jnp.float32),
+            vmem((levels, CORES, rows_mine, tab_dev * embed), tables.dtype),
+            vmem((levels, CORES) + parts_shape[1:], jnp.float32),
+            vmem(tower_weight.shape, tower_weight.dtype),
+            vmem(user_proj.shape, user_proj.dtype),
+            dma((4,)),
+            dma((2, n_cand)),
+            dma((2, n_cand)),
+            dma((n_cand,)),
+            dma((n_cand,)),
+            dma((3,)),
+            dma((3,)),
+            dma((n_table,)),
+            dma((n_table,)),
+            dma((n_table, levels)),
+            dma((n_table, levels)),
         ],
         compiler_params=pltpu.CompilerParams(
-            collective_id=1, has_side_effects=True, vmem_limit_bytes=LIMIT
+            collective_id=0, has_side_effects=True, vmem_limit_bytes=LIMIT
         ),
-        name="rows",
+        name="front",
     )(
-        found.reshape(n_cand, tab_dev * capacity, embed),
-        feats.reshape(requests, user_width),
+        send_rows.reshape(n_cand, per // lanes, lanes),
+        where.reshape(tab_dev * row_total),
+        user_feats,
+        tables.reshape(tab_dev * rows_dev, embed),
         tower_weight,
         tower_bias[None, :],
         user_proj,
@@ -475,44 +547,6 @@
         mlp_second,
         bias_row,
     )
-
-    where = (
-        owner_dev * (tab_dev * capacity)
-        + jnp.arange(tab_dev, dtype=jnp.int32)[:, None] * capacity
-        + slot_pos
-    )
-    fetched = pl.pallas_call(
-        functools.partial(restore_kernel, tab_dev, embed),
-        out_shape=jax.ShapeDtypeStruct((row_total, tab_dev * embed), tables.dtype),
-        in_specs=[SMEM_SPEC, VMEM_SPEC],
-        out_specs=VMEM_SPEC,
-        scratch_shapes=[
-            pltpu.VMEM((slots, embed), jnp.float32),
-            pltpu.VMEM((tab_dev * row_total, embed), jnp.float32),
-        ],
-        compiler_params=pltpu.CompilerParams(vmem_limit_bytes=LIMIT),
-        name="restore",
-    )(where.reshape(tab_dev * row_total), returned.reshape(slots, embed))
-
-    rows_mine = row_total // n_table
-    width = n_table * tab_dev * embed
-    mine, parts = pl.pallas_call(
-        functools.partial(table_kernel, n_table),
-        out_shape=(
-            jax.ShapeDtypeStruct((levels, rows_mine, width), tables.dtype),
-            jax.ShapeDtypeStruct((n_table, levels) + partial.shape[2:], jnp.float32),
-        ),
-        in_specs=[VMEM_SPEC] * 2,
-        out_specs=(VMEM_SPEC,) * 2,
-        scratch_shapes=[
-            pltpu.SemaphoreType.DMA((2, n_table)),
-            pltpu.SemaphoreType.DMA((2, n_table)),
-        ],
-        compiler_params=pltpu.CompilerParams(
-            collective_id=2, has_side_effects=True, vmem_limit_bytes=LIMIT
-        ),
-        name="quarters",
-    )(fetched.reshape(levels, CORES, rows_mine, tab_dev * embed), partial)
 
     tasks = task_weight.shape[1]
     d_top = mlp_second.shape[1]
@@ -549,7 +583,7 @@
             pltpu.SemaphoreType.DMA((levels - 1,)),
         ],
         compiler_params=pltpu.CompilerParams(
-            collective_id=3, has_side_effects=True, vmem_limit_bytes=LIMIT
+            collective_id=1, has_side_effects=True, vmem_limit_bytes=LIMIT
         ),
         name="mlp",
     )(

time: 108 us -> 86.8 us (0.80)
  Pallas kernels: 94.7 us -> 76.3 us
  local copies, waits for them, and re-layouts: 6.79 us -> 5.4 us
    pallas_call x5 -> x1, Pallas kernels: 69 us -> 51.9 us  [on_device(): pl.pallas_call(functools.partial(front_kernel, n_cand, n_table), out_shap...]
    unnamed x13 -> x10, local copies, waits for them, and re-layouts: 2.28 us -> 0.95 us
    pallas_call x1, Pallas kernels: 25.7 us -> 24.4 us  [on_device(): pl.pallas_call(functools.partial(mlp_kernel, n_table, cand_dev), out_shap...]
where the time goes in v3:
time: 86.8 us; the launch traced here: 86.4 us
  Pallas kernels  76.3 us (88%)
  local copies, waits for them, and re-layouts  5.4 us (6%)
  matrix products  3.34 us (4%)
  other arithmetic  1.23 us (1%)
    pallas_call x1, Pallas kernels, on_device(): pl.pallas_call(functools.partial(front_kernel, n_cand, n_table), out_shap...  51.9 us
    pallas_call x1, Pallas kernels, on_device(): pl.pallas_call(functools.partial(mlp_kernel, n_table, cand_dev), out_shap...  24.4 us
    dot_general x2, matrix products, place(): jnp.einsum('tif,tid->tfd', hit, digit_block, preferred_element_type=jnp.f...  3.06 us

profile of v3, /device:TPU:14, one launch (start us, length us, event | category | flops | bytes accessed | tf_op | source)
XLA Modules:
  0.0 86.4 jit_solution(2722496288850471595)
XLA Ops:
  0.0 0.8 reshape.314
  0.8 0.1 convert_reduce_fusion
  1.0 0.3 fusion.10
  1.3 0.8 reshape.315
  2.1 0.1 fusion.24
  2.2 0.1 pad.3.clone
  2.3 0.1 maximum_bitcast_fusion
  2.4 0.0 copy-start
  2.4 3.1 %while.11 = (s32[]{:T(128)}, f32[2,2048,4]{1,2,0:T(4,128)S(1)}, s32[2,2,512]{2,0,1:T(2,128)S(1)}, bf16[2,2,512,4]{2,3,1,0:T(4,128)(2,1)S(1)}, s32[]{:T(128)}, /*index=5*/s32[]{:T(128)}) while((s32[]{:T(128)}, f32[2,2048,4]{1,2,0:T(4,128)S(1)}, s32[2,2,512]{2,0,1:T(2,128)S(1)}, bf16[2,2,512,4]{2,3,1,0:T(4,128)(2,1)S(1)}, s32[]{:T(128)}, ...), condition=%wide.region_4.5_spmd.clone, body=%wide.region_3.4_spmd.clone.sunk | while | flops 18907140 | bytes 159831 | solution.py:460
  2.4 1.5 %fusion.30 = f32[2,2048,4]{1,2,0:T(4,128)S(1)} fusion(s32[2,512]{1,0:T(2,128)S(1)} %bitcast.52, f32[2,2048,4]{1,2,0:T(4,128)S(1)} %get-tuple-element.108, pred[]{:T(512)S(6)} %compare.63, bf16[2,2,512,4]{2,3,1,0:T(4,128)(2,1)S(1)} %get-tuple-element.116, s32[]{:T(128)} %get-tuple-element.107), kind=kOutput, calls=%fused_computation.4.clone.1 | convolution fusion | flops 18907136 | bytes 143365 | tf_op jit(solution)/shard_map/while/body/eval_jaxpr/tif,tid->tfd/dot_general | solution.py:456
  4.0 1.5 %fusion.30 = f32[2,2048,4]{1,2,0:T(4,128)S(1)} fusion(s32[2,512]{1,0:T(2,128)S(1)} %bitcast.52, f32[2,2048,4]{1,2,0:T(4,128)S(1)} %get-tuple-element.108, pred[]{:T(512)S(6)} %compare.63, bf16[2,2,512,4]{2,3,1,0:T(4,128)(2,1)S(1)} %get-tuple-element.116, s32[]{:T(128)} %get-tuple-element.107), kind=kOutput, calls=%fused_computation.4.clone.1 | convolution fusion | flops 18907136 | bytes 143365 | tf_op jit(solution)/shard_map/while/body/eval_jaxpr/tif,tid->tfd/dot_general | solution.py:456
  5.5 0.1 convert_reduce_fusion.1
  5.6 0.1 compare_reduce_fusion
  5.7 0.1 fusion.16
  5.8 0.6 reshape.316.ids
  6.4 0.1 broadcast_bitcast_fusion
  6.5 0.0 copy-done
  6.5 0.1 reshape.317
  6.6 0.6 fusion.20.where
  7.2 0.0 copy-start.1
  7.2 0.0 copy-start.2
  7.2 51.9 %front.1 = (bf16[2,256,1024]{2,1,0:T(8,128)(2,1)}, f32[4,2,4,1024]{3,2,1,0:T(4,128)}, bf16[1024,1024]{1,0:T(8,128)(2,1)}, bf16[1024,1024]{1,0:T(8,128)(2,1)}, f32[1,1024]{1,0:T(1,128)}) custom-call(s32[8,4,128]{2,1,0:T(4,128)} %reshape.316.ids, s32[2048]{0:T(1024)} %fusion.20.where, bf16[2,4096]{1,0:T(2,128)(2,1)} %feats.1, bf16[16384,128]{1,0:T(8,128)(2,1)} %bitcast.51, ...), custom_call_target="tpu_custom_call" | custom-call | tf_op jit(solution)/shard_map/front/pallas_call | solution.py:484
  59.1 0.0 copy-done.1
  59.1 0.8 copy.23.task_w
  60.0 0.0 copy-done.2
  60.0 0.7 copy.24.task_b
  60.6 24.4 %mlp.1 = f32[8,256]{1,0:T(8,128)} custom-call(bf16[2,256,1024]{2,1,0:T(8,128)(2,1)} %get-tuple-element.38.mine, f32[4,2,4,1024]{3,2,1,0:T(4,128)} %get-tuple-element.39.parts, bf16[1024,1024]{1,0:T(8,128)(2,1)} %cross_w.1, f32[1,1024]{1,0:T(1,128)} %bitcast.58, bf16[1024,1024]{1,0:T(8,128)(2,1)} %first.3, bf16[1024,1024]{1,0:T(8,128)(2,1)} %get-tuple-element.40.first_o, ...), custom_call_target="tpu_custom_call" | custom-call | tf_op jit(solution)/shard_map/mlp/pallas_call | solution.py:553
  85.1 1.4 %reshape.319 = f32[8,4,64]{2,1,0:T(4,128)} reshape(f32[8,256]{1,0:T(8,128)} %mlp.1) | data formatting | bytes 16384 | tf_op jit(solution)/shard_map/reshape | solution.py:604
  (16 shorter events, 0.2 us)
Async XLA Ops:
  2.4 4.2 %copy-start = (s32[2,16,64]{2,1,0:T(8,128)S(1)}, s32[2,16,64]{2,1,0:T(8,128)}, u32[]{:S(2)}) copy-start(s32[2,16,64]{2,1,0:T(8,128)} %param.20) | copy-start | bytes 24580
  7.2 51.9 %copy-start.1 = (bf16[1024,8]{0,1:T(8,128)(2,1)S(1)}, bf16[1024,8]{0,1:T(8,128)(2,1)}, u32[]{:S(2)}) copy-start(bf16[1024,8]{0,1:T(8,128)(2,1)} %param.28) | copy-start | bytes 49156
  7.2 52.8 %copy-start.2 = (f32[8]{0:T(128)S(1)}, f32[8]{0:T(128)}, u32[]{:S(2)}) copy-start(f32[8]{0:T(128)} %param.29) | copy-start | bytes 100

commit v4 on v3

--- a/solution.py
+++ b/solution.py
@@ -14,7 +14,7 @@
 ANY_SPEC = pl.BlockSpec(memory_space=pl.ANY)
 STEP = 16
 CORES = 2
-LIMIT = 56 << 20
+LIMIT = 62 << 20
 
 
 def push(src, dst, send, recv, axis, peer):
@@ -53,6 +53,7 @@
 def front_kernel(
     n,
     n_table,
+    cand_dev,
     ids,
     where,
     feats,
@@ -63,11 +64,12 @@
     first,
     second,
     bias,
-    mine,
-    parts,
-    first_o,
-    second_o,
-    bias_o,
+    cross_w,
+    cross_b,
+    second_b,
+    task_w,
+    task_b,
+    out,
     ids_v,
     ids_s,
     feats_v,
@@ -75,14 +77,23 @@
     tab_v,
     wide,
     found,
-    packed,
     returned,
-    ret_wide,
     fetched,
     rows_out,
     partial,
     w_held,
     p_held,
+    mine,
+    parts,
+    cross_v,
+    first_v,
+    second_v,
+    biases,
+    base,
+    crossed,
+    acc,
+    sent,
+    got,
     load,
     id_send,
     id_recv,
@@ -94,6 +105,8 @@
     part_recv,
     q_send,
     q_recv,
+    top_send,
+    top_recv,
 ):
     me = lax.axis_index("cand")
     place = lax.axis_index("table")
@@ -101,9 +114,16 @@
     level = place // CORES
     levels = n_table // CORES
     mate = place + 1 - 2 * core
-    tab_copy = pltpu.make_async_copy(tab, tab_v, load.at[0])
+    tab_copy = pltpu.make_async_copy(tab, tab_v.at[pl.ds(0, tab.shape[0]), :], load.at[0])
     w_copy = pltpu.make_async_copy(tower_w, w_held, load.at[1])
     p_copy = pltpu.make_async_copy(proj_w, p_held, load.at[2])
+    held = [
+        pltpu.make_async_copy(src, dst, load.at[4 + i])
+        for i, (src, dst) in enumerate(
+            ((cross_w, cross_v), (first, first_v.at[0]), (second, second_v.at[0]))
+        )
+    ]
+    per = found.shape[0]
     tab_copy.start()
     barrier = pltpu.get_barrier_semaphore()
     for d in range(1, n):
@@ -129,7 +149,8 @@
 
     def row_copy(d):
         peer = lax.rem(me + d, n)
-        return push(packed.at[peer], returned.at[me], row_send.at[d], row_recv.at[d], "cand", peer)
+        from_here = tab_v.at[pl.ds(pl.multiple_of(peer * per, per), per), :]
+        return push(from_here, returned.at[me], row_send.at[d], row_recv.at[d], "cand", peer)
 
     def each(low, high, act):
         def body(d, carry):
@@ -142,26 +163,29 @@
     each(1, n, lambda d: feat_copy(d).start())
     swaps = [
         push(src, dst, w_send.at[i], w_recv.at[i], "table", mate)
-        for i, (src, dst) in enumerate(((first, first_o), (second, second_o), (bias, bias_o)))
+        for i, (src, dst) in enumerate(
+            ((first, first_v.at[1]), (second, second_v.at[1]), (bias, biases.at[1]))
+        )
     ]
     for copy in swaps:
         copy.start()
+    biases[0] = bias[...]
     ids_v[me] = ids[me]
     feats_v[me] = feats[...]
     tab_copy.wait()
     w_copy.start()
     p_copy.start()
-    widen(tab_v, wide, wide.shape[0])
+    for copy in held:
+        copy.start()
+    widen(tab_v, wide, tab.shape[0])
     each(1, n, lambda d: id_copy(d).wait())
     to_scalar = pltpu.make_async_copy(ids_v, ids_s, load.at[3])
     to_scalar.start()
     to_scalar.wait()
 
-    per = found.shape[0]
     lanes = ids_s.shape[2]
 
-    def gather(d, out):
-        peer = lax.rem(me + d, n)
+    def gather(peer, out):
 
         def body(i, carry):
             at = pl.multiple_of(i * STEP, STEP)
@@ -173,14 +197,15 @@
             return carry
 
         lax.fori_loop(0, per // STEP, body, 0)
-        narrow(found, out.at[peer], per)
+        narrow(found, out, per)
 
     def serve(d):
-        gather(d, packed)
+        peer = lax.rem(me + d, n)
+        gather(peer, tab_v.at[pl.ds(pl.multiple_of(peer * per, per), per), :])
         row_copy(d).start()
 
     each(1, n, serve)
-    gather(0, returned)
+    gather(me, returned.at[me])
 
     each(1, n, lambda d: feat_copy(d).wait())
     step = feats.shape[0]
@@ -198,10 +223,10 @@
             preferred_element_type=jnp.float32,
         )
 
-    acc = lax.fori_loop(
+    summed = lax.fori_loop(
         0, depth // chunk, body, jnp.zeros((feats_f.shape[0], width), jnp.float32)
     )
-    tower = jnp.maximum(acc + tower_b[...], 0.0).astype(jnp.bfloat16)
+    tower = jnp.maximum(summed + tower_b[...], 0.0).astype(jnp.bfloat16)
     p_copy.wait()
     part = jnp.dot(tower, p_held[...], preferred_element_type=jnp.float32)
     quarter = partial.shape[2]
@@ -233,7 +258,7 @@
 
         source = lax.rem(me - d + n, n)
         at = pl.multiple_of(source * per, per)
-        widen(returned.at[source], ret_wide.at[pl.ds(at, per), :], per)
+        widen(returned.at[source], wide.at[pl.ds(at, per), :], per)
 
     each(0, n, arrive)
 
@@ -243,10 +268,11 @@
     share = tab_dev * embed
     lane = pl.ds(pl.multiple_of(place * share, share), share)
     rows = n_table * count
-    quarter_copies = []
-    for turn in range(CORES - 1, -1, -1):
-        target = lax.rem(core + turn, CORES)
-        for y in range(levels):
+    quarter_copies = {}
+    for lv in range(levels):
+        y = lax.rem(level + lv, levels)
+        for turn in range(CORES - 1, -1, -1):
+            target = lax.rem(core + turn, CORES)
             begin = (y * CORES + target) * count
 
             for t in range(tab_dev):
@@ -254,87 +280,41 @@
                 def restore(i, carry):
                     at = pl.multiple_of(i * STEP, STEP)
                     for j in range(STEP):
-                        fetched[pl.ds(at + j, 1), :] = wide_row(t * rows + begin + at + j)
+                        source = where[t * rows + begin + at + j]
+                        fetched[pl.ds(at + j, 1), :] = wide[pl.ds(source, 1), :]
                     return carry
 
-                def wide_row(i):
-                    return ret_wide[pl.ds(where[i], 1), :]
-
                 lax.fori_loop(0, count // STEP, restore, 0)
-                narrow(
-                    fetched, rows_out.at[y, target, :, pl.ds(t * embed, embed)], count
-                )
+                narrow(fetched, rows_out.at[y, target, :, pl.ds(t * embed, embed)], count)
             for up in range(levels - 1, -1, -1):
                 if turn == 0 and up == 0:
                     mine[y, :, lane] = rows_out[y, target]
                     continue
-                peer = lax.rem(level + up, levels) * CORES + target
                 spot = turn * levels + up
                 copy = push(
                     rows_out.at[y, target],
                     mine.at[y, :, lane],
-                    q_send.at[spot, y],
-                    q_recv.at[spot, y],
+                    q_send.at[spot, lv],
+                    q_recv.at[spot, lv],
                     "table",
-                    peer,
+                    lax.rem(level + up, levels) * CORES + target,
                 )
                 copy.start()
-                quarter_copies.append(copy)
-    for copy in quarter_copies + part_copies + swaps:
+                quarter_copies[turn, up, lv] = copy
+
+    for copy in part_copies + swaps:
         copy.wait()
-
-
-def mlp_kernel(
-    n_table,
-    cand_dev,
-    mine,
-    parts,
-    cross_w,
-    cross_b,
-    first,
-    first_o,
-    bias,
-    bias_o,
-    second,
-    second_o,
-    second_b,
-    task_w,
-    task_b,
-    out,
-    cross_v,
-    first_v,
-    second_v,
-    base,
-    crossed,
-    acc,
-    sent,
-    got,
-    load,
-    send,
-    recv,
-):
-    me = lax.axis_index("table")
-    core = lax.rem(me, CORES)
-    level = me // CORES
-    levels = n_table // CORES
-    loads = [pltpu.make_async_copy(cross_w, cross_v, load.at[0])]
-    for i, (one, two) in enumerate(((first, second), (first_o, second_o))):
-        loads.append(pltpu.make_async_copy(one, first_v.at[i], load.at[1 + 2 * i]))
-        loads.append(pltpu.make_async_copy(two, second_v.at[i], load.at[2 + 2 * i]))
-    for copy in loads:
-        copy.start()
-    barrier = pltpu.get_barrier_semaphore()
-    for d in range(1, levels):
-        other = lax.rem(level + d, levels) * CORES + core
-        pl.semaphore_signal(barrier, inc=1, device_id={"table": other}, device_id_type=MESH)
-    pl.semaphore_wait(barrier, levels - 1)
+    for copy in held:
+        copy.wait()
     rows, width = base.shape
     tile = math.gcd(width, 256)
     hidden_tile = math.gcd(first.shape[1], 256)
-    biases = (bias, bias_o)
-    copies = []
+    top_copies = []
     for d in range(1, levels + 1):
         at_level = lax.rem(level + d, levels)
+        for (turn, up, lv), copy in quarter_copies.items():
+            if (d + up) % levels == lv:
+                copy.wait_recv()
         total = parts[0, at_level]
         for q in range(1, n_table):
             total = total + parts[q, at_level]
@@ -344,29 +324,24 @@
             base[span, :] = (
                 mine[at_level, span, :].astype(jnp.float32) + proj[r : r + 1, :]
             ).astype(jnp.bfloat16)
-        if d == 1:
-            loads[0].wait()
 
         def cross(j, carry):
             at = pl.ds(pl.multiple_of(j * tile, tile), tile)
             product = jnp.dot(base[...], cross_v[:, at], preferred_element_type=jnp.float32)
-            wide = base[:, at].astype(jnp.float32)
-            crossed[:, at] = (wide * (product + cross_b[:, at]) + wide).astype(jnp.bfloat16)
+            broad = base[:, at].astype(jnp.float32)
+            crossed[:, at] = (broad * (product + cross_b[:, at]) + broad).astype(jnp.bfloat16)
             return carry
 
         lax.fori_loop(0, width // tile, cross, 0)
         acc[...] = jnp.zeros_like(acc)
         for i in range(CORES):
-            if d == 1:
-                loads[1 + 2 * i].wait()
-                loads[2 + 2 * i].wait()
 
             def layer(j, carry):
                 at = pl.ds(pl.multiple_of(j * hidden_tile, hidden_tile), hidden_tile)
                 hidden = jnp.dot(
                     crossed[...], first_v[i, :, at], preferred_element_type=jnp.float32
                 )
-                hidden = jnp.maximum(hidden + biases[i][:, at], 0.0).astype(jnp.bfloat16)
+                hidden = jnp.maximum(hidden + biases[i, :, at], 0.0).astype(jnp.bfloat16)
                 acc[...] += jnp.dot(
                     hidden, second_v[i, at, :], preferred_element_type=jnp.float32
                 )
@@ -375,27 +350,30 @@
             lax.fori_loop(0, first.shape[1] // hidden_tile, layer, 0)
         if d < levels:
             sent[d - 1] = acc[...].astype(jnp.bfloat16)
-            copies.append(
+            top_copies.append(
                 push(
                     sent.at[d - 1],
                     got.at[d - 1],
-                    send.at[d - 1],
-                    recv.at[d - 1],
+                    top_send.at[d - 1],
+                    top_recv.at[d - 1],
                     "table",
                     at_level * CORES + core,
                 )
             )
-            copies[-1].start()
-    for copy in copies:
+            top_copies[-1].start()
+    for copy in quarter_copies.values():
+        copy.wait_send()
+    for copy in top_copies:
         copy.wait()
     total = acc[...] + second_b[...]
     for d in range(levels - 1):
         total = total + got[d].astype(jnp.float32)
     top = jnp.maximum(total, 0.0).astype(jnp.bfloat16)
     scores = lax.dot_general(
-        task_w[...], top, (((0,), (1,)), ((), ())), preferred_element_type=jnp.float32
-    )
-    out[...] = scores + task_b[...]
+        task_w[...], top, (((1,), (1,)), ((), ())), preferred_element_type=jnp.float32
+    )
+    for k in range(out.shape[0]):
+        out[k : k + 1, :] = scores[k : k + 1, :] + task_b[k]
 
 
 def on_device(
@@ -481,15 +459,12 @@
     parts_shape = (levels, quarter, user_proj.shape[1])
     vmem = pltpu.VMEM
     dma = pltpu.SemaphoreType.DMA
-    mine, parts, first_o, second_o, bias_o = pl.pallas_call(
-        functools.partial(front_kernel, n_cand, n_table),
-        out_shape=(
-            jax.ShapeDtypeStruct((levels, rows_mine, width), tables.dtype),
-            jax.ShapeDtypeStruct((n_table,) + parts_shape, jnp.float32),
-            jax.ShapeDtypeStruct(mlp_first.shape, mlp_first.dtype),
-            jax.ShapeDtypeStruct(mlp_second.shape, mlp_second.dtype),
-            jax.ShapeDtypeStruct(bias_row.shape, bias_row.dtype),
-        ),
+    tasks = task_weight.shape[1]
+    d_top = mlp_second.shape[1]
+    held_rows = max(tab_dev * rows_dev, slots)
+    logits = pl.pallas_call(
+        functools.partial(front_kernel, n_cand, n_table, cand_dev),
+        out_shape=jax.ShapeDtypeStruct((tasks, rows_mine), jnp.float32),
         in_specs=[
             VMEM_SPEC,
             SMEM_SPEC,
@@ -501,25 +476,39 @@
             ANY_SPEC,
             ANY_SPEC,
             VMEM_SPEC,
+            ANY_SPEC,
+            VMEM_SPEC,
+            VMEM_SPEC,
+            VMEM_SPEC,
+            SMEM_SPEC,
         ],
-        out_specs=(VMEM_SPEC, VMEM_SPEC, ANY_SPEC, ANY_SPEC, VMEM_SPEC),
+        out_specs=VMEM_SPEC,
         scratch_shapes=[
             vmem((n_cand, per // lanes, lanes), jnp.int32),
             pltpu.SMEM((n_cand, per // lanes, lanes), jnp.int32),
             vmem((n_cand, req_dev, user_width), user_feats.dtype),
             vmem((requests, user_width), jnp.float32),
-            vmem((tab_dev * rows_dev, embed), tables.dtype),
-            vmem((tab_dev * rows_dev, embed), jnp.float32),
+            vmem((held_rows, embed), tables.dtype),
+            vmem((held_rows, embed), jnp.float32),
             vmem((per, embed), jnp.float32),
             vmem((n_cand, per, embed), tables.dtype),
-            vmem((n_cand, per, embed), tables.dtype),
-            vmem((slots, embed), jnp.float32),
             vmem((rows_mine, embed), jnp.float32),
             vmem((levels, CORES, rows_mine, tab_dev * embed), tables.dtype),
             vmem((levels, CORES) + parts_shape[1:], jnp.float32),
             vmem(tower_weight.shape, tower_weight.dtype),
             vmem(user_proj.shape, user_proj.dtype),
-            dma((4,)),
+            vmem((levels, rows_mine, width), tables.dtype),
+            vmem((n_table,) + parts_shape, jnp.float32),
+            vmem(cross_weight.shape, cross_weight.dtype),
+            vmem((CORES,) + mlp_first.shape, mlp_first.dtype),
+            vmem((CORES,) + mlp_second.shape, mlp_second.dtype),
+            vmem((CORES,) + bias_row.shape, bias_row.dtype),
+            vmem((rows_mine, width), jnp.bfloat16),
+            vmem((rows_mine, width), jnp.bfloat16),
+            vmem((rows_mine, d_top), jnp.float32),
+            vmem((levels - 1, rows_mine, d_top), jnp.bfloat16),
+            vmem((levels - 1, rows_mine, d_top), jnp.bfloat16),
+            dma((7,)),
             dma((2, n_cand)),
             dma((2, n_cand)),
             dma((n_cand,)),
@@ -530,11 +519,13 @@
             dma((n_table,)),
             dma((n_table, levels)),
             dma((n_table, levels)),
+            dma((levels - 1,)),
+            dma((levels - 1,)),
         ],
         compiler_params=pltpu.CompilerParams(
             collective_id=0, has_side_effects=True, vmem_limit_bytes=LIMIT
         ),
-        name="front",
+        name="whole",
     )(
         send_rows.reshape(n_cand, per // lanes, lanes),
         where.reshape(tab_dev * row_total),
@@ -546,60 +537,11 @@
         mlp_first,
         mlp_second,
         bias_row,
-    )
-
-    tasks = task_weight.shape[1]
-    d_top = mlp_second.shape[1]
-    logits = pl.pallas_call(
-        functools.partial(mlp_kernel, n_table, cand_dev),
-        out_shape=jax.ShapeDtypeStruct((tasks, rows_mine), jnp.float32),
-        in_specs=[
-            VMEM_SPEC,
-            VMEM_SPEC,
-            ANY_SPEC,
-            VMEM_SPEC,
-            ANY_SPEC,
-            ANY_SPEC,
-            VMEM_SPEC,
-            VMEM_SPEC,
-            ANY_SPEC,
-            ANY_SPEC,
-            VMEM_SPEC,
-            VMEM_SPEC,
-            VMEM_SPEC,
-        ],
-        out_specs=VMEM_SPEC,
-        scratch_shapes=[
-            pltpu.VMEM(cross_weight.shape, cross_weight.dtype),
-            pltpu.VMEM((CORES,) + mlp_first.shape, mlp_first.dtype),
-            pltpu.VMEM((CORES,) + mlp_second.shape, mlp_second.dtype),
-            pltpu.VMEM((rows_mine, width), jnp.bfloat16),
-            pltpu.VMEM((rows_mine, width), jnp.bfloat16),
-            pltpu.VMEM((rows_mine, d_top), jnp.float32),
-            pltpu.VMEM((levels - 1, rows_mine, d_top), jnp.bfloat16),
-            pltpu.VMEM((levels - 1, rows_mine, d_top), jnp.bfloat16),
-            pltpu.SemaphoreType.DMA((1 + 2 * CORES,)),
-            pltpu.SemaphoreType.DMA((levels - 1,)),
-            pltpu.SemaphoreType.DMA((levels - 1,)),
-        ],
-        compiler_params=pltpu.CompilerParams(
-            collective_id=1, has_side_effects=True, vmem_limit_bytes=LIMIT
-        ),
-        name="mlp",
-    )(
-        mine,
-        parts,
         cross_weight,
         cross_bias[None, :],
-        mlp_first,
-        first_o,
-        bias_row,
-        bias_o,
-        mlp_second,
-        second_o,
         second_bias[None, :],
-        task_weight,
-        task_bias[:, None],
+        task_weight.T,
+        task_bias,
     )
     return logits.reshape(tasks, requests // n_table, cand_dev)
 

time: 86.8 us -> 75.7 us (0.87)
  Pallas kernels: 76.3 us -> 66.7 us
  local copies, waits for them, and re-layouts: 5.4 us -> 3.88 us
    pallas_call x2 -> x1, Pallas kernels: 76.3 us -> 66.7 us  [on_device(): pl.pallas_call(functools.partial(front_kernel, n_cand, n_table, cand_dev)...]
where the time goes in v4:
time: 75.7 us; the launch traced here: 75.3 us
  Pallas kernels  66.7 us (88%)
  local copies, waits for them, and re-layouts  3.88 us (5%)
  matrix products  3.34 us (4%)
  other arithmetic  1.24 us (2%)
    pallas_call x1, Pallas kernels, on_device(): pl.pallas_call(functools.partial(front_kernel, n_cand, n_table, cand_dev)...  66.7 us
    dot_general x2, matrix products, place(): jnp.einsum('tif,tid->tfd', hit, digit_block, preferred_element_type=jnp.f...  3.06 us
    reshape x3, local copies, waits for them, and re-layouts, on_device(): flat_ids = item_ids.reshape(tab_dev, row_total)  1.66 us

profile of v4, /device:TPU:14, one launch (start us, length us, event | category | flops | bytes accessed | tf_op | source)
XLA Modules:
  0.0 75.3 jit_solution(8000271868921591493)
XLA Ops:
  0.0 0.8 %reshape.314 = s32[2,2,512]{2,1,0:T(2,128)S(1)} reshape(s32[2,16,64]{2,1,0:T(8,128)} %param.20) | data formatting | bytes 16384 | tf_op jit(solution)/shard_map/reshape | solution.py:405
  0.8 0.1 convert_reduce_fusion
  1.0 0.3 fusion.10
  1.3 0.8 %reshape.315 = s32[2,2,512,1]{2,1,0,3:T(2,128)S(1)} reshape(s32[2,16,64]{2,1,0:T(8,128)} %param.20) | data formatting | bytes 16384 | tf_op jit(solution)/shard_map/reshape | solution.py:405
  2.1 0.1 fusion.24
  2.2 0.1 pad.3.clone
  2.3 0.1 maximum_bitcast_fusion
  2.4 0.0 copy-start
  2.4 3.1 %while.11 = (s32[]{:T(128)}, f32[2,2048,4]{1,2,0:T(4,128)S(1)}, s32[2,2,512]{2,0,1:T(2,128)S(1)}, bf16[2,2,512,4]{2,3,1,0:T(4,128)(2,1)S(1)}, s32[]{:T(128)}, /*index=5*/s32[]{:T(128)}) while((s32[]{:T(128)}, f32[2,2048,4]{1,2,0:T(4,128)S(1)}, s32[2,2,512]{2,0,1:T(2,128)S(1)}, bf16[2,2,512,4]{2,3,1,0:T(4,128)(2,1)S(1)}, s32[]{:T(128)}, ...), condition=%wide.region_4.5_spmd.clone, body=%wide.region_3.4_spmd.clone.sunk | while | flops 18907140 | bytes 159831 | solution.py:438
  2.4 1.5 %fusion.30 = f32[2,2048,4]{1,2,0:T(4,128)S(1)} fusion(s32[2,512]{1,0:T(2,128)S(1)} %bitcast.52, f32[2,2048,4]{1,2,0:T(4,128)S(1)} %get-tuple-element.98, pred[]{:T(512)S(6)} %compare.63, bf16[2,2,512,4]{2,3,1,0:T(4,128)(2,1)S(1)} %get-tuple-element.106, s32[]{:T(128)} %get-tuple-element.97), kind=kOutput, calls=%fused_computation.4.clone.1 | convolution fusion | flops 18907136 | bytes 143365 | tf_op jit(solution)/shard_map/while/body/eval_jaxpr/tif,tid->tfd/dot_general | solution.py:434
  4.0 1.5 %fusion.30 = f32[2,2048,4]{1,2,0:T(4,128)S(1)} fusion(s32[2,512]{1,0:T(2,128)S(1)} %bitcast.52, f32[2,2048,4]{1,2,0:T(4,128)S(1)} %get-tuple-element.98, pred[]{:T(512)S(6)} %compare.63, bf16[2,2,512,4]{2,3,1,0:T(4,128)(2,1)S(1)} %get-tuple-element.106, s32[]{:T(128)} %get-tuple-element.97), kind=kOutput, calls=%fused_computation.4.clone.1 | convolution fusion | flops 18907136 | bytes 143365 | tf_op jit(solution)/shard_map/while/body/eval_jaxpr/tif,tid->tfd/dot_general | solution.py:434
  5.5 0.1 convert_reduce_fusion.1
  5.6 0.1 compare_reduce_fusion
  5.7 0.1 fusion.16
  5.8 0.6 reshape.316.ids
  6.4 0.1 broadcast_bitcast_fusion
  6.5 0.0 copy-done
  6.5 0.1 reshape.317
  6.6 0.6 fusion.20.where
  7.2 66.7 %whole.1 = f32[8,256]{1,0:T(8,128)} custom-call(s32[8,4,128]{2,1,0:T(4,128)} %reshape.316.ids, s32[2048]{0:T(1024)} %fusion.20.where, bf16[2,4096]{1,0:T(2,128)(2,1)} %feats.1, bf16[16384,128]{1,0:T(8,128)(2,1)} %bitcast.51, bf16[4096,1024]{1,0:T(8,128)(2,1)} %tower_w.1, f32[1,1024]{1,0:T(1,128)} %bitcast.57, bf16[1024,1024]{1,0:T(8,128)(2,1)} %proj_w.1, ...), custom_call_target="tpu_custom_call" | custom-call | tf_op jit(solution)/shard_map/whole/pallas_call | solution.py:465
  73.9 1.4 %reshape.319 = f32[8,4,64]{2,1,0:T(4,128)} reshape(f32[8,256]{1,0:T(8,128)} %whole.1) | data formatting | bytes 16384 | tf_op jit(solution)/shard_map/reshape | solution.py:546
  (16 shorter events, 0.2 us)
Async XLA Ops:
  2.4 4.2 %copy-start = (s32[2,16,64]{2,1,0:T(8,128)S(1)}, s32[2,16,64]{2,1,0:T(8,128)}, u32[]{:S(2)}) copy-start(s32[2,16,64]{2,1,0:T(8,128)} %param.20) | copy-start | bytes 24580

commit v5 on v4

--- a/solution.py
+++ b/solution.py
@@ -309,6 +309,8 @@
     rows, width = base.shape
     tile = math.gcd(width, 256)
     hidden_tile = math.gcd(first.shape[1], 256)
+    units, d_top = second.shape
+    top_tile = math.gcd(d_top, 256)
     top_copies = []
     for d in range(1, levels + 1):
         at_level = lax.rem(level + d, levels)
@@ -333,7 +335,6 @@
             return carry
 
         lax.fori_loop(0, width // tile, cross, 0)
-        acc[...] = jnp.zeros_like(acc)
         for i in range(CORES):
 
             def layer(j, carry):
@@ -341,21 +342,32 @@
                 hidden = jnp.dot(
                     crossed[...], first_v[i, :, at], preferred_element_type=jnp.float32
                 )
-                hidden = jnp.maximum(hidden + biases[i, :, at], 0.0).astype(jnp.bfloat16)
-                acc[...] += jnp.dot(
-                    hidden, second_v[i, at, :], preferred_element_type=jnp.float32
+                hidden = jnp.maximum(hidden + biases[i, :, at], 0.0)
+                w_held[i * rows : (i + 1) * rows, at] = hidden.astype(jnp.bfloat16)
+                return carry
+
+            lax.fori_loop(0, units // hidden_tile, layer, 0)
+        for c in range(d_top // top_tile):
+            at = slice(c * top_tile, (c + 1) * top_tile)
+            term = jnp.dot(
+                w_held[0:rows, 0:units], second_v[0, :, at], preferred_element_type=jnp.float32
+            )
+            for i in range(1, CORES):
+                term += jnp.dot(
+                    w_held[i * rows : (i + 1) * rows, 0:units],
+                    second_v[i, :, at],
+                    preferred_element_type=jnp.float32,
                 )
-                return carry
-
-            lax.fori_loop(0, first.shape[1] // hidden_tile, layer, 0)
-        if d < levels:
-            sent[d - 1] = acc[...].astype(jnp.bfloat16)
+            if d == levels:
+                acc[:, at] = term
+                continue
+            sent[d - 1, :, at] = term.astype(jnp.bfloat16)
             top_copies.append(
                 push(
-                    sent.at[d - 1],
-                    got.at[d - 1],
-                    top_send.at[d - 1],
-                    top_recv.at[d - 1],
+                    sent.at[d - 1, :, at],
+                    got.at[d - 1, :, at],
+                    top_send.at[d - 1, c],
+                    top_recv.at[d - 1, c],
                     "table",
                     at_level * CORES + core,
                 )
@@ -519,8 +531,8 @@
             dma((n_table,)),
             dma((n_table, levels)),
             dma((n_table, levels)),
-            dma((levels - 1,)),
-            dma((levels - 1,)),
+            dma((levels - 1, d_top // math.gcd(d_top, 256))),
+            dma((levels - 1, d_top // math.gcd(d_top, 256))),
         ],
         compiler_params=pltpu.CompilerParams(
             collective_id=0, has_side_effects=True, vmem_limit_bytes=LIMIT

time: 75.7 us -> 73.1 us (0.966)
  Pallas kernels: 66.7 us -> 63.9 us
    pallas_call x1, Pallas kernels: 66.7 us -> 63.9 us  [on_device(): pl.pallas_call(functools.partial(front_kernel, n_cand, n_table, cand_dev)...]
where the time goes in v5:
time: 73.1 us; the launch traced here: 72.5 us
  Pallas kernels  63.9 us (87%)
  local copies, waits for them, and re-layouts  3.88 us (5%)
  matrix products  3.34 us (5%)
  other arithmetic  1.24 us (2%)
    pallas_call x1, Pallas kernels, on_device(): pl.pallas_call(functools.partial(front_kernel, n_cand, n_table, cand_dev)...  63.9 us
    dot_general x2, matrix products, place(): jnp.einsum('tif,tid->tfd', hit, digit_block, preferred_element_type=jnp.f...  3.06 us
    reshape x3, local copies, waits for them, and re-layouts, on_device(): flat_ids = item_ids.reshape(tab_dev, row_total)  1.66 us

profile of v5, /device:TPU:14, one launch (start us, length us, event | category | flops | bytes accessed | tf_op | source)
XLA Modules:
  0.0 72.5 jit_solution(3654089319523271791)
XLA Ops:
  0.0 0.8 %reshape.314 = s32[2,2,512]{2,1,0:T(2,128)S(1)} reshape(s32[2,16,64]{2,1,0:T(8,128)} %param.20) | data formatting | bytes 16384 | tf_op jit(solution)/shard_map/reshape | solution.py:417
  0.8 0.1 convert_reduce_fusion
  1.0 0.3 fusion.10
  1.3 0.8 %reshape.315 = s32[2,2,512,1]{2,1,0,3:T(2,128)S(1)} reshape(s32[2,16,64]{2,1,0:T(8,128)} %param.20) | data formatting | bytes 16384 | tf_op jit(solution)/shard_map/reshape | solution.py:417
  2.1 0.1 fusion.24
  2.2 0.1 pad.3.clone
  2.3 0.1 maximum_bitcast_fusion
  2.4 0.0 copy-start
  2.4 3.1 %while.11 = (s32[]{:T(128)}, f32[2,2048,4]{1,2,0:T(4,128)S(1)}, s32[2,2,512]{2,0,1:T(2,128)S(1)}, bf16[2,2,512,4]{2,3,1,0:T(4,128)(2,1)S(1)}, s32[]{:T(128)}, /*index=5*/s32[]{:T(128)}) while((s32[]{:T(128)}, f32[2,2048,4]{1,2,0:T(4,128)S(1)}, s32[2,2,512]{2,0,1:T(2,128)S(1)}, bf16[2,2,512,4]{2,3,1,0:T(4,128)(2,1)S(1)}, s32[]{:T(128)}, ...), condition=%wide.region_4.5_spmd.clone, body=%wide.region_3.4_spmd.clone.sunk | while | flops 18907140 | bytes 159831 | solution.py:450
  2.4 1.5 %fusion.30 = f32[2,2048,4]{1,2,0:T(4,128)S(1)} fusion(s32[2,512]{1,0:T(2,128)S(1)} %bitcast.52, f32[2,2048,4]{1,2,0:T(4,128)S(1)} %get-tuple-element.98, pred[]{:T(512)S(6)} %compare.63, bf16[2,2,512,4]{2,3,1,0:T(4,128)(2,1)S(1)} %get-tuple-element.106, s32[]{:T(128)} %get-tuple-element.97), kind=kOutput, calls=%fused_computation.4.clone.1 | convolution fusion | flops 18907136 | bytes 143365 | tf_op jit(solution)/shard_map/while/body/eval_jaxpr/tif,tid->tfd/dot_general | solution.py:446
  4.0 1.5 %fusion.30 = f32[2,2048,4]{1,2,0:T(4,128)S(1)} fusion(s32[2,512]{1,0:T(2,128)S(1)} %bitcast.52, f32[2,2048,4]{1,2,0:T(4,128)S(1)} %get-tuple-element.98, pred[]{:T(512)S(6)} %compare.63, bf16[2,2,512,4]{2,3,1,0:T(4,128)(2,1)S(1)} %get-tuple-element.106, s32[]{:T(128)} %get-tuple-element.97), kind=kOutput, calls=%fused_computation.4.clone.1 | convolution fusion | flops 18907136 | bytes 143365 | tf_op jit(solution)/shard_map/while/body/eval_jaxpr/tif,tid->tfd/dot_general | solution.py:446
  5.5 0.1 convert_reduce_fusion.1
  5.6 0.1 compare_reduce_fusion
  5.7 0.1 fusion.16
  5.8 0.6 reshape.316.ids
  6.4 0.1 broadcast_bitcast_fusion
  6.5 0.0 copy-done
  6.5 0.1 reshape.317
  6.6 0.6 fusion.20.where
  7.2 63.9 %whole.1 = f32[8,256]{1,0:T(8,128)} custom-call(s32[8,4,128]{2,1,0:T(4,128)} %reshape.316.ids, s32[2048]{0:T(1024)} %fusion.20.where, bf16[2,4096]{1,0:T(2,128)(2,1)} %feats.1, bf16[16384,128]{1,0:T(8,128)(2,1)} %bitcast.51, bf16[4096,1024]{1,0:T(8,128)(2,1)} %tower_w.1, f32[1,1024]{1,0:T(1,128)} %bitcast.57, bf16[1024,1024]{1,0:T(8,128)(2,1)} %proj_w.1, ...), custom_call_target="tpu_custom_call" | custom-call | tf_op jit(solution)/shard_map/whole/pallas_call | solution.py:477
  71.1 1.4 %reshape.319 = f32[8,4,64]{2,1,0:T(4,128)} reshape(f32[8,256]{1,0:T(8,128)} %whole.1) | data formatting | bytes 16384 | tf_op jit(solution)/shard_map/reshape | solution.py:558
  (16 shorter events, 0.2 us)
Async XLA Ops:
  2.4 4.2 %copy-start = (s32[2,16,64]{2,1,0:T(8,128)S(1)}, s32[2,16,64]{2,1,0:T(8,128)}, u32[]{:S(2)}) copy-start(s32[2,16,64]{2,1,0:T(8,128)} %param.20) | copy-start | bytes 24580
